TPU v7x, 32 devices: a whole 2x2x4 slice. The times are simulated.
32 devices in a mesh: scene: 2 (over y), seq: 4 (over z), head: 2 (over x), band: 2 (over core).
Axes of the slice: x: 2, y: 2, z: 4, core: 2. Of those that a mesh axis runs over, the one named last changes fastest.
Arguments:
- tokens: bfloat16 [8, 12, 37, 1024], P(('scene', 'seq'), ('head', 'band')), parts along dimension 0, may hold values from -6 to 6
- frame_gain: float32 [1024], replicated, may hold values from 0.5 to 1.5
- frame_qkv: bfloat16 [3, 1024, 1024], P(None, None, 'head'), may hold values from -6 to 6
- frame_out: bfloat16 [1024, 1024], P('head'), may hold values from -0.1875 to 0.1875
- global_gain: float32 [1024], replicated, may hold values from 0.5 to 1.5
- global_qkv: bfloat16 [3, 1024, 1024], P(None, None, 'head'), may hold values from -6 to 6
- global_out: bfloat16 [1024, 1024], P('head'), may hold values from -0.1875 to 0.1875
- head_gain: float32 [2048], replicated, may hold values from 0.5 to 1.5
- head_proj: bfloat16 [2048, 256], replicated, may hold values from -0.125 to 0.125
- head_bias: float32 [256], replicated, may hold values from -3 to 3
- head_conv: bfloat16 [3, 3, 256, 256], replicated, may hold values from -0.125 to 0.125
Outputs:
- blocks: bfloat16 [8, 12, 37, 1024], P(('scene', 'seq'), ('head', 'band')), parts along dimension 0
- features: bfloat16 [8, 12, 37, 256], P(('scene', 'seq'), ('head', 'band')), parts along dimension 0
There are 2 independent parts, one for each index of `scene`. A program takes and returns all parts, laid end to end along the dimension named above; an argument that names none is the same for every part. Nothing has to cross between parts.
All inputs are finite; a program needn't handle non-finite values.
Results may differ from a plain program's by a relative error of at most 0.017.
Values may be sent and summed in bfloat16 or wider, within the bound.
A program may use at most 256 MiB of HBM per device.

v0:
```python
import functools

import jax
import jax.numpy as jnp
from jax import lax
from jax.experimental import pallas as pl
from jax.experimental.pallas import tpu as pltpu
from jax.sharding import PartitionSpec as P

HD = 64


norm_eps = 1e-06
head_eps = 1e-05


def padded_2(block, sides, width):
    for axis, dim in sides:
        count = lax.axis_size(axis)
        forward = [(i, i + 1) for i in range(count - 1)]
        backward = [(target, source) for source, target in forward]
        low = lax.ppermute(
            lax.slice_in_dim(block, block.shape[dim] - width, None, axis=dim), axis, forward
        )
        high = lax.ppermute(lax.slice_in_dim(block, 0, width, axis=dim), axis, backward)
        block = jnp.concatenate([low, block, high], axis=dim)
    return block


def layer_norm(values, gain, epsilon):
    centre = values - jnp.mean(values, axis=-1, keepdims=True)
    spread = jnp.mean(centre * centre, axis=-1, keepdims=True)
    return centre * lax.rsqrt(spread + epsilon) * gain


def by_heads(matrix):
    return matrix.reshape(matrix.shape[0], matrix.shape[1] // HD, HD)


def attend_local(queries, keys_all, values_all):
    scores = jnp.einsum(
        "qhd,khd->qhk", by_heads(queries), by_heads(keys_all), preferred_element_type=jnp.float32
    ) * HD ** (-0.5)
    probs = jnp.exp(scores - jnp.max(scores, axis=-1, keepdims=True))
    mixed = jnp.einsum(
        "qhk,khd->qhd",
        probs.astype(jnp.bfloat16),
        by_heads(values_all),
        preferred_element_type=jnp.float32,
    )
    mixed = mixed / jnp.sum(probs, axis=-1)[..., None]
    return mixed.reshape(queries.shape).astype(jnp.bfloat16)


def key_step(local_rows, portion_rows):
    amount = portion_rows // local_rows
    best = 1
    for factor in range(1, amount + 1):
        if amount % factor == 0 and local_rows * factor <= max(local_rows, 1024):
            best = factor
    return local_rows * best


def fresh_carry(queries):
    heads_q = by_heads(queries)
    return (
        jnp.full(heads_q.shape[:2], -jnp.inf, jnp.float32),
        jnp.zeros(heads_q.shape[:2], jnp.float32),
        jnp.zeros(heads_q.shape, jnp.float32),
    )


def finish(carry, queries):
    return (carry[2] / carry[1][..., None]).reshape(queries.shape).astype(jnp.bfloat16)


def fold_keys(queries, carry, portions, local_rows):
    keys_in, values_in = portions
    step_rows = key_step(local_rows, keys_in.shape[0])
    heads_q = by_heads(queries)
    key_blocks = keys_in.reshape(-1, step_rows, keys_in.shape[1])
    value_blocks = values_in.reshape(-1, step_rows, values_in.shape[1])

    def absorb(states, blocks_pair):
        running_max, running_sum, weighted = states
        scores = jnp.einsum(
            "qhd,khd->qhk", heads_q, by_heads(blocks_pair[0]), preferred_element_type=jnp.float32
        ) * HD ** (-0.5)
        new_max = jnp.maximum(running_max, jnp.max(scores, axis=-1))
        decay = jnp.exp(running_max - new_max)
        probs = jnp.exp(scores - new_max[..., None])
        running_sum = running_sum * decay + jnp.sum(probs, axis=-1)
        weighted = weighted * decay[..., None] + jnp.einsum(
            "qhk,khd->qhd",
            probs.astype(jnp.bfloat16),
            by_heads(blocks_pair[1]),
            preferred_element_type=jnp.float32,
        )
        return ((new_max, running_sum, weighted), None)

    carry, ignored = lax.scan(absorb, carry, (key_blocks, value_blocks))
    return carry


def attention_block(inputs, gain, qkv_weight, out_weight, wide):
    normed = layer_norm(inputs.astype(jnp.float32), gain, norm_eps).astype(jnp.bfloat16)
    gathered = lax.all_gather(normed, "head", axis=1, tiled=True)
    flattened = gathered.reshape(-1, gathered.shape[-1])
    query_rows = jnp.dot(flattened, qkv_weight[0], preferred_element_type=jnp.float32).astype(
        jnp.bfloat16
    )
    key_rows = jnp.dot(flattened, qkv_weight[1], preferred_element_type=jnp.float32).astype(
        jnp.bfloat16
    )
    value_rows = jnp.dot(flattened, qkv_weight[2], preferred_element_type=jnp.float32).astype(
        jnp.bfloat16
    )
    if wide:
        carry = fold_keys(
            query_rows,
            fresh_carry(query_rows),
            (
                lax.all_gather(key_rows, ("seq", "band"), axis=0, tiled=True),
                lax.all_gather(value_rows, ("seq", "band"), axis=0, tiled=True),
            ),
            key_rows.shape[0],
        )
        attended = finish(carry, query_rows)
    else:
        keys_all, values_all = (
            lax.all_gather(key_rows, "band", axis=0, tiled=True),
            lax.all_gather(value_rows, "band", axis=0, tiled=True),
        )
        attended = attend_local(query_rows, keys_all, values_all)
    band_rows = inputs.shape[1] * inputs.shape[2]
    own_rows = lax.all_to_all(attended, "head", split_axis=0, concat_axis=1, tiled=True)
    branch = jnp.dot(
        own_rows,
        lax.all_gather(out_weight, "head", axis=0, tiled=True),
        preferred_element_type=jnp.float32,
    )
    merged = inputs.astype(jnp.float32).reshape(band_rows, -1) + branch
    return merged.astype(jnp.bfloat16).reshape(inputs.shape)


def on_device(
    tokens,
    frame_gain,
    frame_qkv,
    frame_out,
    global_gain,
    global_qkv,
    global_out,
    head_gain,
    head_proj,
    head_bias,
    head_conv,
):
    first = attention_block(tokens, frame_gain, frame_qkv, frame_out, False)
    second = attention_block(first, global_gain, global_qkv, global_out, True)
    band_height = tokens.shape[1]
    grid_width = tokens.shape[2]
    stacked = jnp.concatenate([first.astype(jnp.float32), second.astype(jnp.float32)], axis=-1)
    normed = layer_norm(stacked, head_gain, head_eps).astype(jnp.bfloat16)
    projected = (
        jnp.dot(
            normed.reshape(-1, stacked.shape[-1]), head_proj, preferred_element_type=jnp.float32
        )
        + head_bias
    )
    projected = projected.astype(jnp.bfloat16).reshape(
        tokens.shape[0], band_height, grid_width, head_proj.shape[1]
    )
    padded = padded_2(projected, ((("head", "band"), 1),), 1)
    padded = jnp.pad(padded, ((0, 0), (0, 0), (1, 1), (0, 0)))
    totals = jnp.zeros(projected.shape, jnp.float32)
    for offset_row in range(3):
        for offset_col in range(3):
            window = padded[
                :, offset_row : offset_row + band_height, offset_col : offset_col + grid_width
            ]
            totals = totals + jnp.einsum(
                "frcx,xy->frcy",
                window,
                head_conv[offset_row, offset_col],
                preferred_element_type=jnp.float32,
            )
    return (second, totals.astype(jnp.bfloat16))


BF = jnp.bfloat16
F32 = jnp.float32
TILE = 16


def up(count):
    return -(-count // TILE) * TILE


def mm(a, b):
    return jnp.dot(a, b, preferred_element_type=F32)


def swap(values):
    return pltpu.roll(values, HD, axis=1)


def scene_kernel(
    seq,
    real,
    width,
    tok,
    f_gain,
    f_qkv,
    f_out,
    g_gain,
    g_qkv,
    g_out,
    h_gain,
    h_proj,
    h_bias,
    h_conv,
    blocks_ref,
    feat_ref,
    toks,
    wf,
    wg,
    fo,
    go,
    wp,
    wc,
    q1,
    k1,
    v1,
    att,
    acc,
    normed,
    sqk,
    sv,
    rqk,
    rv,
    kk,
    vx,
    so,
    ro,
    a2,
    r2,
    pj,
    halo,
    xbuf,
    send,
    recv,
    local,
):
    s, z = lax.axis_index("scene"), lax.axis_index("seq")
    x, c = lax.axis_index("head"), lax.axis_index("band")
    rows, dim = tok.shape
    cols = wf.shape[2]
    pairs = cols // (2 * HD)
    frame = 4 * rows
    half = frame // 2
    peers = [None, (s, z, x, 1 - c), (s, z, 1 - x, c), (s, z, 1 - x, 1 - c)]

    def z_peer(offset):
        return (s, lax.rem(z + offset, seq), x, c)

    started = []

    def put(index, source, target, device):
        copy = pltpu.make_async_remote_copy(
            src_ref=source,
            dst_ref=target,
            send_sem=send.at[index],
            recv_sem=recv.at[index],
            device_id=device,
            device_id_type=pl.DeviceIdType.MESH,
        )
        copy.start()
        started.append(copy)
        return copy

    own_cols = pl.ds(pl.multiple_of(c * cols, cols), cols)
    other_cols = pl.ds(pl.multiple_of((1 - c) * cols, cols), cols)
    loads = [
        pltpu.make_async_copy(f_qkv.at[:, :, own_cols], wf, local.at[0]),
        pltpu.make_async_copy(f_out.at[own_cols], fo.at[0], local.at[1]),
        pltpu.make_async_copy(f_out.at[other_cols], fo.at[1], local.at[2]),
        pltpu.make_async_copy(g_qkv.at[:, :, own_cols], wg, local.at[3]),
        pltpu.make_async_copy(g_out.at[own_cols], go.at[0], local.at[4]),
        pltpu.make_async_copy(g_out.at[other_cols], go.at[1], local.at[5]),
        pltpu.make_async_copy(h_proj, wp, local.at[6]),
        pltpu.make_async_copy(h_conv, wc, local.at[7]),
    ]
    for load in loads:
        load.start()

    barrier = pltpu.get_barrier_semaphore()
    everyone = peers[1:] + [z_peer(d) for d in range(1, seq)]
    for device in everyone:
        pl.semaphore_signal(
            barrier, inc=1, device_id=device, device_id_type=pl.DeviceIdType.MESH
        )
    pl.semaphore_wait(barrier, len(everyone))

    T_CORE, T_X, T_FWD, F_X, F_Z, F_FWD, G_X, G_FWD = 0, 1, 2, 3, 5, 7, 9, 10
    A_CORE, A_X, A_FWD = 11, 11 + pairs, 11 + 2 * pairs
    ZQ = 11 + 3 * pairs
    ZV, ZO = ZQ + seq, ZQ + 2 * seq
    B2 = ZQ + 3 * seq
    HALO = B2 + 4

    tok_x = put(T_X, tok, toks.at[2], peers[2])
    tok_core = put(T_CORE, tok, toks.at[1], peers[1])
    mine = lax.rem(z, 2)
    part = cols // 2
    chunk = part // 2

    def piece(owner, k):
        return pl.ds(pl.multiple_of(owner * part + k * chunk, chunk), chunk)

    fo_x = []
    for k in range(2):
        source = f_out.at[pl.ds(pl.multiple_of(c * cols + mine * part + k * chunk, chunk), chunk)]
        fo_x.append(put(F_X + k, source, fo.at[2, piece(mine, k)], peers[2]))

    block_row = lax.broadcasted_iota(jnp.int32, (rows, 1), 0)
    block_valid = block_row < real
    valid = jnp.concatenate([block_valid] * 4, axis=0)
    low = lax.broadcasted_iota(jnp.int32, (1, 2 * HD), 1) < HD

    def qkv1(slot, source):
        n = layer_norm(source[...].astype(F32), f_gain[...], norm_eps).astype(BF)
        at = pl.ds(slot * rows, rows)
        q1[at, :] = (mm(n, wf[0]).astype(BF) * HD ** (-0.5)).astype(BF)
        k1[at, :] = mm(n, wf[1]).astype(BF)
        v1[at, :] = jnp.where(block_valid, mm(n, wf[2]), 0.0).astype(BF)

    loads[0].wait()
    qkv1(0, tok)
    tok_core.wait_recv()
    qkv1(1, toks.at[1])
    tok_x.wait_recv()
    tok_fwd = put(T_FWD, toks.at[2], toks.at[3], peers[1])
    qkv1(2, toks.at[2])
    tok_fwd.wait_recv()
    qkv1(3, toks.at[3])

    att_core, att_x = [], []
    ones = jnp.where(valid, 1.0, 0.0).astype(BF)
    for p in range(pairs):
        at = pl.ds(p * 2 * HD, 2 * HD)
        qp, kp, vp = q1[:, at], k1[:, at], v1[:, at]
        outs = []
        for keep in (low, jnp.logical_not(low)):
            scores = lax.dot_general(
                jnp.where(keep, qp, jnp.zeros_like(qp)),
                kp,
                (((1,), (1,)), ((), ())),
                preferred_element_type=F32,
            )
            probs = jnp.exp(scores - jnp.max(scores, axis=-1, keepdims=True))
            outs.append(mm(probs.astype(BF), jnp.where(keep, vp, ones)))
        top = jnp.where(low, outs[0], outs[1])
        bottom = swap(jnp.where(low, outs[1], outs[0]))
        att[0, p] = (top / bottom).astype(BF)
        att_x.append(put(A_X + p, att.at[0, p], att.at[2, p], peers[2]))
        att_core.append(put(A_CORE + p, att.at[0, p], att.at[1, p], peers[1]))
    pair_peer = (s, z + 1 - 2 * mine, x, c)
    mine_rows = pl.ds(pl.multiple_of(mine * part, part), part)
    pair_rows = pl.ds(pl.multiple_of((1 - mine) * part, part), part)
    fo_z = []
    for k in range(2):
        fo_x[k].wait_recv()
        at = piece(mine, k)
        fo_z.append(put(F_Z + k, fo.at[2, at], fo.at[2, at], pair_peer))
    fo_fwd = [put(F_FWD, fo.at[2, mine_rows], fo.at[3, mine_rows], peers[1])]
    go_x = put(G_X, g_out.at[own_cols], go.at[2], peers[2])

    def gathered(group):
        parts = []
        for r in group:
            for p in range(pairs):
                parts.append(
                    jnp.concatenate(
                        [att[r, p, pl.ds((r ^ t) * rows, rows), :] for t in range(4)], axis=0
                    )
                )
        return jnp.concatenate(parts, axis=1)

    steps = dim // 256

    def column(i):
        return pl.ds(pl.multiple_of(i * 256, 256), 256)

    for load in loads[1:3]:
        load.wait()
    for copy in att_core:
        copy.wait_recv()
    lhs_near = gathered((0, 1))

    @pl.loop(0, steps)
    def _(i):
        at = column(i)
        weight = jnp.concatenate([fo[0, :, at], fo[1, :, at]], axis=0)
        base = jnp.concatenate(
            [tok[:, at]] + [toks[r, :, at] for r in (1, 2, 3)], axis=0
        ).astype(F32)
        acc[:, at] = base + mm(lhs_near, weight)

    for copy in fo_z:
        copy.wait_recv()
    fo_fwd.append(put(F_FWD + 1, fo.at[2, pair_rows], fo.at[3, pair_rows], peers[1]))
    att_fwd = []
    for p in range(pairs):
        att_x[p].wait_recv()
        att_fwd.append(put(A_FWD + p, att.at[2, p], att.at[3, p], peers[1]))
    for copy in fo_fwd + att_fwd:
        copy.wait_recv()
    lhs_far = gathered((2, 3))

    @pl.loop(0, steps)
    def _(i):
        at = column(i)
        weight = jnp.concatenate([fo[2, :, at], fo[3, :, at]], axis=0)
        acc[:, at] += mm(lhs_far, weight)

    for t in range(4):
        at = pl.ds(t * rows, rows)
        first = acc[at, :].astype(BF).astype(F32)
        normed[at, :] = layer_norm(first, g_gain[...], norm_eps).astype(BF)
    loads[3].wait()
    n2 = normed[...]
    for p in range(pairs):
        at = pl.ds(p * 2 * HD, 2 * HD)
        qp = (mm(n2, wg[0, :, at]).astype(BF) * HD ** (-0.5)).astype(F32)
        kp = mm(n2, wg[1, :, at])
        vp = jnp.where(valid, mm(n2, wg[2, :, at]), 0.0)
        sqk[2 * p] = jnp.where(low, qp, swap(kp)).astype(BF)
        sqk[2 * p + 1] = jnp.where(low, swap(qp), kp).astype(BF)
        upper, under = vp[:half], vp[half:]
        sv[2 * p] = jnp.where(low, upper, swap(under)).astype(BF)
        sv[2 * p + 1] = jnp.where(low, swap(upper), under).astype(BF)

    z_copies = []
    for d in range(1, seq):
        to = lax.rem(z + d, seq)
        z_copies.append(put(ZQ + d, sqk.at[to], rqk.at[d], z_peer(d)))
        z_copies.append(put(ZV + d, sv.at[to], rv.at[d], z_peer(d)))
    rqk[0] = sqk[z]
    rv[0] = sv[z]

    go_x.wait_recv()
    go_fwd = put(G_FWD, go.at[2], go.at[3], peers[1])

    def arrange(d):
        at = pl.ds(d * frame, frame)
        kk[at, :] = swap(rqk[d].astype(F32)).astype(BF)
        packed = rv[d].astype(F32)
        spread = jnp.concatenate([packed, swap(packed)], axis=0)
        vx[at, :] = jnp.where(low, spread, jnp.where(valid, 1.0, 0.0)).astype(BF)

    arrange(0)
    for d in range(1, seq):
        z_copies[2 * d - 2].wait_recv()
        z_copies[2 * d - 1].wait_recv()
        arrange(d)

    def back(d):
        return pltpu.make_async_remote_copy(
            src_ref=so.at[d],
            dst_ref=ro.at[z],
            send_sem=send.at[ZO + d],
            recv_sem=recv.at[ZO + d],
            device_id=z_peer(seq - d),
            device_id_type=pl.DeviceIdType.MESH,
        )

    @pl.loop(1, seq + 1)
    def _(i):
        d = lax.rem(i, seq)
        keys, values = kk[...], vx[...]
        outs = []
        for part in range(2):
            qp = rqk[d, pl.ds(part * half, half), :]
            scores = lax.dot_general(
                jnp.where(low, qp, jnp.zeros_like(qp)),
                keys,
                (((1,), (1,)), ((), ())),
                preferred_element_type=F32,
            )
            probs = jnp.exp(scores - jnp.max(scores, axis=-1, keepdims=True))
            mixed = mm(probs.astype(BF), values)
            outs.append(mixed / jnp.where(low, swap(mixed), 1.0))
        so[d] = jnp.where(low, outs[0], swap(outs[1])).astype(BF)

        @pl.when(d > 0)
        def _():
            back(d).start()

    ro[z] = so[0]
    for d in range(1, seq):
        back(d).wait_recv()

    for p in range(pairs):
        at = pl.ds(p * 2 * HD, 2 * HD)
        even, odd = ro[2 * p].astype(F32), ro[2 * p + 1].astype(F32)
        a2[pl.ds(0, half), at] = jnp.where(low, even, swap(odd)).astype(BF)
        a2[pl.ds(half, half), at] = jnp.where(low, swap(even), odd).astype(BF)
    a2_copies = [
        put(B2 + r, a2.at[pl.ds(r * rows, rows)], r2.at[r], peers[r]) for r in (2, 3, 1)
    ]
    own = pl.ds(0, rows)
    first = acc[own, :].astype(BF).astype(F32)
    for load in loads[4:]:
        load.wait()
    go_fwd.wait_recv()
    branch = mm(a2[own, :], go[0])
    for copy in a2_copies:
        copy.wait_recv()
    for r in range(1, 4):
        branch = branch + mm(r2[r], go[r])
    second = (first + branch).astype(BF)
    blocks_ref[...] = second
    stacked = jnp.concatenate([first, second.astype(F32)], axis=-1)
    n3 = layer_norm(stacked, h_gain[...], head_eps).astype(BF)
    pj[...] = (mm(n3, wp[...]) + h_bias[...]).astype(BF)

    place = 2 * x + c
    after = lax.rem(place + 1, 4)
    before = lax.rem(place + 3, 4)

    def frame_peer(index):
        return (s, z, index // 2, lax.rem(index, 2))

    start = (real - width) // TILE * TILE
    slab = halo.shape[1]
    down = put(HALO, pj.at[pl.ds(start, rows - start)], halo.at[0, pl.ds(0, rows - start)], frame_peer(after))
    upward = put(HALO + 1, pj.at[pl.ds(0, slab)], halo.at[1], frame_peer(before))
    base = 8
    xbuf[...] = jnp.zeros_like(xbuf)
    xbuf[base + width : base + width + real, :] = pj[...].astype(F32)[:real]
    down.wait_recv()
    upward.wait_recv()
    skip = real - width - start
    lower = jnp.where(place > 0, halo[0].astype(F32), 0.0)
    upper = jnp.where(place < 3, halo[1].astype(F32), 0.0)
    xbuf[base : base + width, :] = lower[skip : skip + width]
    xbuf[base + width + real : base + 2 * width + real, :] = upper[:width]
    col = lax.rem(block_row, width)
    total = jnp.zeros(feat_ref.shape, F32)
    for i in range(3):
        for j in range(3):
            first_row = base + width * i + j - 1
            window = xbuf[first_row : first_row + rows, :]
            if j == 0:
                window = jnp.where(col > 0, window, 0.0)
            if j == 2:
                window = jnp.where(col < width - 1, window, 0.0)
            total = total + mm(window.astype(BF), wc[3 * i + j])
    feat_ref[...] = total.astype(BF)

    for copy in started:
        copy.wait_send()
    for d in range(1, seq):
        back(d).wait_send()


def scene_program(seq, *arrays):
    (tokens, f_gain, f_qkv, f_out, g_gain, g_qkv, g_out, h_gain, h_proj, h_bias, h_conv) = arrays
    height, width, dim = tokens.shape[1:]
    real = height * width
    rows = up(real)
    cols = f_qkv.shape[2] // 2
    pairs = cols // (2 * HD)
    channels = h_proj.shape[1]
    frame = 4 * rows
    half = frame // 2
    flat = tokens.reshape(real, dim)
    flat = jnp.concatenate([flat] + [flat[-1:]] * (rows - real), axis=0)
    vmem = pl.BlockSpec(memory_space=pltpu.VMEM)
    hbm = pl.BlockSpec(memory_space=pl.ANY)
    start = (real - width) // TILE * TILE
    slab = max(up(width), rows - start)
    copies = 11 + 3 * pairs + 3 * seq + 4 + 2
    blocks, features = pl.pallas_call(
        functools.partial(scene_kernel, seq, real, width),
        out_shape=(
            jax.ShapeDtypeStruct((rows, dim), BF),
            jax.ShapeDtypeStruct((rows, channels), BF),
        ),
        in_specs=[vmem, vmem, hbm, hbm, vmem, hbm, hbm, vmem, hbm, vmem, hbm],
        out_specs=(vmem, vmem),
        scratch_shapes=[
            pltpu.VMEM((4, rows, dim), BF),
            pltpu.VMEM((3, dim, cols), BF),
            pltpu.VMEM((3, dim, cols), BF),
            pltpu.VMEM((4, cols, dim), BF),
            pltpu.VMEM((4, cols, dim), BF),
            pltpu.VMEM(h_proj.shape, BF),
            pltpu.VMEM((9, channels, channels), BF),
            pltpu.VMEM((frame, cols), BF),
            pltpu.VMEM((frame, cols), BF),
            pltpu.VMEM((frame, cols), BF),
            pltpu.VMEM((4, pairs, frame, 2 * HD), BF),
            pltpu.VMEM((frame, dim), F32),
            pltpu.VMEM((frame, dim), BF),
            pltpu.VMEM((seq, frame, 2 * HD), BF),
            pltpu.VMEM((seq, half, 2 * HD), BF),
            pltpu.VMEM((seq, frame, 2 * HD), BF),
            pltpu.VMEM((seq, half, 2 * HD), BF),
            pltpu.VMEM((seq * frame, 2 * HD), BF),
            pltpu.VMEM((seq * frame, 2 * HD), BF),
            pltpu.VMEM((seq, half, 2 * HD), BF),
            pltpu.VMEM((seq, half, 2 * HD), BF),
            pltpu.VMEM((frame, cols), BF),
            pltpu.VMEM((4, rows, cols), BF),
            pltpu.VMEM((rows, channels), BF),
            pltpu.VMEM((2, slab, channels), BF),
            pltpu.VMEM((up(rows + 2 * width + 2 * TILE), channels), F32),
            pltpu.SemaphoreType.DMA((copies,)),
            pltpu.SemaphoreType.DMA((copies,)),
            pltpu.SemaphoreType.DMA((8,)),
        ],
        compiler_params=pltpu.CompilerParams(
            collective_id=0, has_side_effects=True
        ),
    )(
        flat,
        f_gain.reshape(1, -1),
        f_qkv,
        f_out,
        g_gain.reshape(1, -1),
        g_qkv,
        g_out,
        h_gain.reshape(1, -1),
        h_proj,
        h_bias.reshape(1, -1),
        h_conv.reshape(9, channels, channels),
    )
    return (
        blocks[:real].reshape(tokens.shape),
        features[:real].reshape(1, height, width, channels),
    )


def routed(mesh, *arrays):
    sizes = mesh.shape
    frames, height, width = arrays[0].shape[:3]
    heads = arrays[2].shape[2] // HD
    fits = (
        sizes["head"] == 2
        and sizes["band"] == 2
        and frames == 1
        and heads == 2 * sizes["seq"]
        and sizes["seq"] % 2 == 0
        and arrays[2].shape[2] // 2 % (4 * TILE) == 0
        and height * width >= up(width)
    )
    if fits:
        return scene_program(sizes["seq"], *arrays)
    return on_device(*arrays)


def solution(mesh):
    return jax.shard_map(
        functools.partial(routed, mesh),
        mesh=mesh,
        in_specs=(
            P(("scene", "seq"), ("head", "band"), None, None),
            P(),
            P(None, None, "head"),
            P("head", None),
            P(),
            P(None, None, "head"),
            P("head", None),
            P(),
            P(),
            P(),
            P(),
        ),
        out_specs=(
            P(("scene", "seq"), ("head", "band"), None, None),
            P(("scene", "seq"), ("head", "band"), None, None),
        ),
        check_vma=False,
    )
```

profile of v0, /device:TPU:0, one launch (start us, length us, event | category | flops | bytes accessed | tf_op | source)
XLA Modules:
  0.0 71.4 jit_solution(4602917196053961597)
XLA Ops:
  0.6 1.0 %reshape.28 = bf16[111,1024]{1,0:T(8,128)(2,1)S(1)} reshape(bf16[1,3,37,1024]{3,2,1,0:T(8,128)(2,1)} %param.11) | data formatting | bytes 454656 | tf_op jit(solution)/shard_map/reshape | solution.py:578
  1.7 0.7 pad_maximum_fusion.tok
  2.4 65.9 %shard_map.122 = (bf16[112,1024]{1,0:T(8,128)(2,1)}, bf16[112,256]{1,0:T(8,128)(2,1)}) custom-call(bf16[112,1024]{1,0:T(8,128)(2,1)} %pad_maximum_fusion.tok, f32[1,1024]{1,0:T(1,128)} %bitcast.11, bf16[3,1024,512]{2,1,0:T(8,128)(2,1)} %f_qkv.1, bf16[512,1024]{1,0:T(8,128)(2,1)} %f_out.1, f32[1,1024]{1,0:T(1,128)} %bitcast.12, bf16[3,1024,512]{2,1,0:T(8,128)(2,1)} %g_qkv.1, ...), custom_call_target="tpu_custom_call" | custom-call | tf_op jit(solution)/shard_map/pallas_call | solution.py:585
  68.3 1.7 %reshape.34 = bf16[1,3,37,1024]{3,2,1,0:T(8,128)(2,1)} reshape(bf16[111,1024]{1,0:T(8,128)(2,1)} %bitcast.8) | data formatting | bytes 454656 | tf_op jit(solution)/shard_map/reshape | solution.py:641
  70.0 1.5 %reshape.35 = bf16[1,3,37,256]{3,2,1,0:T(8,128)(2,1)} reshape(bf16[111,256]{1,0:T(8,128)(2,1)} %bitcast.9) | data formatting | bytes 113664 | tf_op jit(solution)/shard_map/reshape | solution.py:642
  (1 shorter events, 0.0 us)
where the time goes:
time: 71.7 us; the launch traced here: 71.4 us
  Pallas kernels  65.9 us (92%)
  local copies, waits for them, and re-layouts  4.17 us (6%)
    pallas_call x1, Pallas kernels, scene_program(): pl.pallas_call(functools.partial(scene_kernel, seq, real, width), out_sha...  65.9 us
    reshape x1, local copies, waits for them, and re-layouts, scene_program(): blocks[:real].reshape(tokens.shape)  1.69 us
    reshape x1, local copies, waits for them, and re-layouts, scene_program(): features[:real].reshape(1, height, width, channels)  1.46 us

commit v1 on v0

v1 whole, which is shorter than its diff:
```python
import functools
import math

import jax
import jax.numpy as jnp
from jax import lax
from jax.experimental import pallas as pl
from jax.experimental.pallas import tpu as pltpu
from jax.sharding import PartitionSpec as P

HD = 64


norm_eps = 1e-06
head_eps = 1e-05


def padded_2(block, sides, width):
    for axis, dim in sides:
        count = lax.axis_size(axis)
        forward = [(i, i + 1) for i in range(count - 1)]
        backward = [(target, source) for source, target in forward]
        low = lax.ppermute(
            lax.slice_in_dim(block, block.shape[dim] - width, None, axis=dim), axis, forward
        )
        high = lax.ppermute(lax.slice_in_dim(block, 0, width, axis=dim), axis, backward)
        block = jnp.concatenate([low, block, high], axis=dim)
    return block


def layer_norm(values, gain, epsilon):
    centre = values - jnp.mean(values, axis=-1, keepdims=True)
    spread = jnp.mean(centre * centre, axis=-1, keepdims=True)
    return centre * lax.rsqrt(spread + epsilon) * gain


def by_heads(matrix):
    return matrix.reshape(matrix.shape[0], matrix.shape[1] // HD, HD)


def attend_local(queries, keys_all, values_all):
    scores = jnp.einsum(
        "qhd,khd->qhk", by_heads(queries), by_heads(keys_all), preferred_element_type=jnp.float32
    ) * HD ** (-0.5)
    probs = jnp.exp(scores - jnp.max(scores, axis=-1, keepdims=True))
    mixed = jnp.einsum(
        "qhk,khd->qhd",
        probs.astype(jnp.bfloat16),
        by_heads(values_all),
        preferred_element_type=jnp.float32,
    )
    mixed = mixed / jnp.sum(probs, axis=-1)[..., None]
    return mixed.reshape(queries.shape).astype(jnp.bfloat16)


def key_step(local_rows, portion_rows):
    amount = portion_rows // local_rows
    best = 1
    for factor in range(1, amount + 1):
        if amount % factor == 0 and local_rows * factor <= max(local_rows, 1024):
            best = factor
    return local_rows * best


def fresh_carry(queries):
    heads_q = by_heads(queries)
    return (
        jnp.full(heads_q.shape[:2], -jnp.inf, jnp.float32),
        jnp.zeros(heads_q.shape[:2], jnp.float32),
        jnp.zeros(heads_q.shape, jnp.float32),
    )


def finish(carry, queries):
    return (carry[2] / carry[1][..., None]).reshape(queries.shape).astype(jnp.bfloat16)


def fold_keys(queries, carry, portions, local_rows):
    keys_in, values_in = portions
    step_rows = key_step(local_rows, keys_in.shape[0])
    heads_q = by_heads(queries)
    key_blocks = keys_in.reshape(-1, step_rows, keys_in.shape[1])
    value_blocks = values_in.reshape(-1, step_rows, values_in.shape[1])

    def absorb(states, blocks_pair):
        running_max, running_sum, weighted = states
        scores = jnp.einsum(
            "qhd,khd->qhk", heads_q, by_heads(blocks_pair[0]), preferred_element_type=jnp.float32
        ) * HD ** (-0.5)
        new_max = jnp.maximum(running_max, jnp.max(scores, axis=-1))
        decay = jnp.exp(running_max - new_max)
        probs = jnp.exp(scores - new_max[..., None])
        running_sum = running_sum * decay + jnp.sum(probs, axis=-1)
        weighted = weighted * decay[..., None] + jnp.einsum(
            "qhk,khd->qhd",
            probs.astype(jnp.bfloat16),
            by_heads(blocks_pair[1]),
            preferred_element_type=jnp.float32,
        )
        return ((new_max, running_sum, weighted), None)

    carry, ignored = lax.scan(absorb, carry, (key_blocks, value_blocks))
    return carry


def attention_block(inputs, gain, qkv_weight, out_weight, wide):
    normed = layer_norm(inputs.astype(jnp.float32), gain, norm_eps).astype(jnp.bfloat16)
    gathered = lax.all_gather(normed, "head", axis=1, tiled=True)
    flattened = gathered.reshape(-1, gathered.shape[-1])
    query_rows = jnp.dot(flattened, qkv_weight[0], preferred_element_type=jnp.float32).astype(
        jnp.bfloat16
    )
    key_rows = jnp.dot(flattened, qkv_weight[1], preferred_element_type=jnp.float32).astype(
        jnp.bfloat16
    )
    value_rows = jnp.dot(flattened, qkv_weight[2], preferred_element_type=jnp.float32).astype(
        jnp.bfloat16
    )
    if wide:
        carry = fold_keys(
            query_rows,
            fresh_carry(query_rows),
            (
                lax.all_gather(key_rows, ("seq", "band"), axis=0, tiled=True),
                lax.all_gather(value_rows, ("seq", "band"), axis=0, tiled=True),
            ),
            key_rows.shape[0],
        )
        attended = finish(carry, query_rows)
    else:
        keys_all, values_all = (
            lax.all_gather(key_rows, "band", axis=0, tiled=True),
            lax.all_gather(value_rows, "band", axis=0, tiled=True),
        )
        attended = attend_local(query_rows, keys_all, values_all)
    band_rows = inputs.shape[1] * inputs.shape[2]
    own_rows = lax.all_to_all(attended, "head", split_axis=0, concat_axis=1, tiled=True)
    branch = jnp.dot(
        own_rows,
        lax.all_gather(out_weight, "head", axis=0, tiled=True),
        preferred_element_type=jnp.float32,
    )
    merged = inputs.astype(jnp.float32).reshape(band_rows, -1) + branch
    return merged.astype(jnp.bfloat16).reshape(inputs.shape)


def on_device(
    tokens,
    frame_gain,
    frame_qkv,
    frame_out,
    global_gain,
    global_qkv,
    global_out,
    head_gain,
    head_proj,
    head_bias,
    head_conv,
):
    first = attention_block(tokens, frame_gain, frame_qkv, frame_out, False)
    second = attention_block(first, global_gain, global_qkv, global_out, True)
    band_height = tokens.shape[1]
    grid_width = tokens.shape[2]
    stacked = jnp.concatenate([first.astype(jnp.float32), second.astype(jnp.float32)], axis=-1)
    normed = layer_norm(stacked, head_gain, head_eps).astype(jnp.bfloat16)
    projected = (
        jnp.dot(
            normed.reshape(-1, stacked.shape[-1]), head_proj, preferred_element_type=jnp.float32
        )
        + head_bias
    )
    projected = projected.astype(jnp.bfloat16).reshape(
        tokens.shape[0], band_height, grid_width, head_proj.shape[1]
    )
    padded = padded_2(projected, ((("head", "band"), 1),), 1)
    padded = jnp.pad(padded, ((0, 0), (0, 0), (1, 1), (0, 0)))
    totals = jnp.zeros(projected.shape, jnp.float32)
    for offset_row in range(3):
        for offset_col in range(3):
            window = padded[
                :, offset_row : offset_row + band_height, offset_col : offset_col + grid_width
            ]
            totals = totals + jnp.einsum(
                "frcx,xy->frcy",
                window,
                head_conv[offset_row, offset_col],
                preferred_element_type=jnp.float32,
            )
    return (second, totals.astype(jnp.bfloat16))


BF = jnp.bfloat16
F32 = jnp.float32
TILE = 16
LANES = 2 * HD
QSCALE = HD ** (-0.5) * math.log2(math.e)


def up(count):
    return -(-count // TILE) * TILE


def mm(a, b):
    return jnp.dot(a, b, preferred_element_type=F32)


def swap(values):
    return pltpu.roll(values, HD, axis=1)


def dot_t(a, b):
    return lax.dot_general(a, b, (((1,), (1,)), ((), ())), preferred_element_type=F32)


def row_parts(rows):
    first = up(rows // 2)
    return [(0, first), (first, rows - first)]


def step_list(rows):
    steps, at = [], 0
    for j in range(2):
        for start, size in row_parts(rows):
            steps.append((j, start, size, at))
            at += 2 * size
    return steps


def sem_layout(seq, pairs):
    names = [
        ("tok", 1), ("tok_x", 2), ("tok_f", 2), ("att", 4), ("part", 4), ("norm", 4),
        ("kv", 4 * seq), ("q", 4 * seq), ("o", 4 * seq), ("go", 2), ("halo", 2),
    ]
    at, table = 0, {}
    for name, size in names:
        table[name] = at
        at += size
    return table, at


def scene_kernel(
    seq,
    height,
    width,
    tok_ref,
    f_gain,
    f_qkv,
    f_out,
    g_gain,
    g_qkv,
    g_out,
    h_gain,
    h_proj,
    h_bias,
    h_conv,
    blocks_ref,
    feat_ref,
    stage,
    toks,
    wf,
    wg,
    wkv1,
    wkv2,
    fo,
    go,
    wp,
    wc,
    q1,
    kv1,
    vx1,
    att,
    att_in,
    p_own,
    p_out,
    p_in,
    n_own,
    n_in,
    fst,
    q2,
    skv,
    kv,
    vx,
    sq,
    rq,
    so,
    ro,
    a2,
    pj,
    halo,
    xbuf,
    send,
    recv,
    local,
):
    s, z = lax.axis_index("scene"), lax.axis_index("seq")
    x, c = lax.axis_index("head"), lax.axis_index("band")
    real = height * width
    rows, dim = fst.shape
    cols = wf.shape[2]
    pairs = cols // LANES
    frame = 4 * rows
    half = rows // 2
    steps = step_list(rows)
    parts = row_parts(rows)
    sems, _ = sem_layout(seq, pairs)
    core, across = (s, z, x, 1 - c), (s, z, 1 - x, c)
    place = 2 * x + c

    def z_peer(offset):
        return (s, lax.rem(z + offset, seq), x, c)

    def remote(name, index, source, target, device, back=None):
        return pltpu.make_async_remote_copy(
            src_ref=source,
            dst_ref=target,
            send_sem=send.at[sems[name] + index],
            recv_sem=recv.at[sems[name] + (index if back is None else back)],
            device_id=device,
            device_id_type=pl.DeviceIdType.MESH,
        )

    started = []

    def put(name, index, source, target, device):
        copy = remote(name, index, source, target, device)
        copy.start()
        started.append(copy)
        return copy

    own_cols = pl.ds(pl.multiple_of(c * cols, cols), cols)
    loads = []

    def load(source, target):
        copy = pltpu.make_async_copy(source, target, local.at[len(loads)])
        copy.start()
        loads.append(copy)
        return copy

    wf_load = load(f_qkv.at[:, :, own_cols], wf)
    fo_loads = []
    for r in range(2):
        owner = c if r == 0 else 1 - c
        for i in range(2 * pairs):
            source = f_out.at[pl.ds(pl.multiple_of(owner * cols + i * HD, HD), HD)]
            fo_loads.append(load(source, fo.at[pl.ds(r * cols + (i ^ 1) * HD, HD)]))
    wg_load = load(g_qkv.at[:, :, own_cols], wg)
    half_rows = pl.ds(pl.multiple_of(x * 2 * cols, 2 * cols), 2 * cols)
    late_loads = [load(g_out, go.at[half_rows]), load(h_proj, wp), load(h_conv, wc)]

    barrier = pltpu.get_barrier_semaphore()
    everyone = [core, across, (s, z, 1 - x, 1 - c)] + [z_peer(d) for d in range(1, seq)]
    for device in everyone:
        pl.semaphore_signal(
            barrier, inc=1, device_id=device, device_id_type=pl.DeviceIdType.MESH
        )
    for r in range(height):
        stage[r * width : (r + 1) * width, :] = tok_ref[0, r].astype(F32)
    for r in range(real, rows):
        stage[r : r + 1, :] = stage[real - 1 : real, :]
    toks[0] = stage[0:rows, :].astype(BF)
    pl.semaphore_wait(barrier, len(everyone))

    tok_x = []
    for k, (start, size) in enumerate(parts):
        at = pl.ds(start, size)
        tok_x.append(put("tok_x", k, toks.at[0, at], toks.at[2, at], across))
    tok_core = put("tok", 0, toks.at[0], toks.at[1], core)

    low = lax.broadcasted_iota(jnp.int32, (1, LANES), 1) < HD
    lane = lax.broadcasted_iota(jnp.int32, (1, 2 * cols), 1)
    v_lanes = lax.rem(lax.div(lane, HD), 4)
    v_lanes = jnp.logical_or(v_lanes == 1, v_lanes == 2)

    def valid_rows(start, size):
        return lax.broadcasted_iota(jnp.int32, (size, 1), 0) + start < real

    wf_load.wait()
    for p in range(pairs):
        at = pl.ds(p * LANES, LANES)
        k_part, v_part = wf[1, :, at], swap(wf[2, :, at].astype(F32)).astype(BF)
        wkv1[:, pl.ds(2 * p * LANES, LANES)] = jnp.where(low, k_part, v_part)
        wkv1[:, pl.ds((2 * p + 1) * LANES, LANES)] = jnp.where(low, v_part, k_part)

    def qkv1(slot, start, size, band):
        n = layer_norm(toks[slot, pl.ds(start, size)].astype(F32), f_gain[...], norm_eps).astype(BF)
        at = pl.ds(pl.multiple_of(band * rows + start, TILE), size)
        q1[at, :] = (mm(n, wf[0]) * QSCALE).astype(BF)
        both = mm(n, wkv1[...]).astype(BF)
        kv1[at, :] = both
        one = jnp.where(v_lanes, both, jnp.ones_like(both))
        vx1[at, :] = jnp.where(valid_rows(start, size), one, jnp.zeros_like(one))

    qkv1(0, 0, rows, place)
    tok_core.wait_recv()
    qkv1(1, 0, rows, 2 * x + 1 - c)
    wg_load.wait()
    for p in range(pairs):
        at = pl.ds(p * LANES, LANES)
        k_part, v_part = wg[1, :, at], wg[2, :, at]
        k_swap, v_swap = swap(k_part.astype(F32)).astype(BF), swap(v_part.astype(F32)).astype(BF)
        wkv2[:, pl.ds(2 * p * LANES, LANES)] = jnp.where(low, k_part, v_swap)
        wkv2[:, pl.ds((2 * p + 1) * LANES, LANES)] = jnp.where(low, k_swap, v_part)
    tok_f = []
    for k, (start, size) in enumerate(parts):
        at = pl.ds(start, size)
        tok_x[k].wait_recv()
        tok_f.append(put("tok_f", k, toks.at[2, at], toks.at[3, at], core))
        qkv1(2, start, size, 2 * (1 - x) + c)
    for k, (start, size) in enumerate(parts):
        tok_f[k].wait_recv()
        qkv1(3, start, size, 2 * (1 - x) + 1 - c)

    att_copies, p_copies, n_copies = [], [], []

    def attend(k):
        j, start, size, _ = steps[k]
        for p in range(pairs):
            at = pl.ds(p * LANES, LANES)
            qp = jnp.concatenate(
                [q1[pl.ds((2 * j + b) * rows + start, size), at] for b in range(2)], axis=0
            )
            mixed = []
            for e in range(2):
                tile = pl.ds((2 * p + e) * LANES, LANES)
                zero = jnp.zeros_like(qp)
                lhs = jnp.where(low, qp, zero) if e == 0 else jnp.where(low, zero, qp)
                scores = dot_t(lhs, kv1[:, tile])
                probs = jnp.exp2(scores - jnp.max(scores, axis=-1, keepdims=True))
                mixed.append(mm(probs.astype(BF), vx1[:, tile]))
            top = jnp.where(low, mixed[1], mixed[0])
            bottom = swap(jnp.where(low, mixed[0], mixed[1]))
            out = (top / bottom).astype(BF)
            for b in range(2):
                att[k, b, pl.ds(0, size), at] = out[b * size : (b + 1) * size]
        at = pl.ds(0, size)
        att_copies.append(put("att", k, att.at[k, 1 - c, at], att_in.at[k, at], core))

    def project(k):
        j, start, size, _ = steps[k]
        at = pl.ds(0, size)
        att_copies[k].wait_recv()
        lhs = jnp.concatenate([att[k, c, at], att_in[k, at]], axis=1)
        partial = mm(lhs, fo[...])
        p_own[k, at] = partial
        p_out[k, at] = partial.astype(BF)
        p_copies.append(put("part", k, p_out.at[k, at], p_in.at[k, at], across))

    def norm2(k):
        j, start, size, _ = steps[k]
        at = pl.ds(0, size)
        slot = jnp.where(x == j, 0, 2)
        p_copies[k].wait_recv()
        tok = toks[slot, pl.ds(start, size)].astype(F32)
        first = (tok + p_own[k, at] + p_in[k, at].astype(F32)).astype(BF)

        @pl.when(x == j)
        def _():
            fst[pl.ds(start, size), :] = first

        n_own[k, at] = layer_norm(first.astype(F32), g_gain[...], norm_eps).astype(BF)
        n_copies.append(put("norm", k, n_own.at[k, at], n_in.at[k, at], core))

    kv_copies, q_copies = [], []
    base_row = pl.multiple_of(z * frame, frame)

    def qkv2(k):
        j, start, size, offset = steps[k]
        n_copies[k].wait_recv()
        at = pl.ds(0, size)
        n = jnp.concatenate([n_own[k, at], n_in[k, at]], axis=0)
        both = mm(n, wkv2[...]).astype(BF)
        for h in range(2 * pairs):
            skv[h, pl.ds(offset, 2 * size), :] = both[:, h * LANES : (h + 1) * LANES]
        to = pl.ds(pl.multiple_of(z * frame + offset, TILE), 2 * size)
        for d in range(1, seq):
            peer = lax.rem(z + d, seq)
            kv_copies.append(
                put("kv", k * seq + d, skv.at[peer, pl.ds(offset, 2 * size)], kv.at[to], z_peer(d))
            )
        kv[to, :] = skv[z, pl.ds(offset, 2 * size), :]
        queries = mm(n, wg[0]) * QSCALE
        q2[2 * j + c, pl.ds(start, size), :] = queries[:size]
        q2[2 * j + 1 - c, pl.ds(start, size), :] = queries[size:]

    for copy in fo_loads:
        copy.wait()
    attend(0)
    attend(1)
    project(0)
    attend(2)
    project(1)
    attend(3)
    project(2)
    project(3)
    go_part = pl.ds(pl.multiple_of(x * 2 * cols + c * cols, cols), cols)
    go_from = pl.ds(pl.multiple_of((1 - x) * 2 * cols + c * cols, cols), cols)
    go_x = put("go", 0, g_out.at[own_cols], go.at[go_part], across)
    norm2(0)
    norm2(1)
    qkv2(0)
    qkv2(1)
    norm2(2)
    norm2(3)
    qkv2(2)
    qkv2(3)
    for b in range(4):
        for p in range(pairs):
            tile = q2[b, :, pl.ds(p * LANES, LANES)]
            top, under = tile[:half], tile[half:]
            sq[2 * p, b] = jnp.where(low, top, swap(under)).astype(BF)
            sq[2 * p + 1, b] = jnp.where(low, swap(top), under).astype(BF)
        for d in range(1, seq):
            peer = lax.rem(z + d, seq)
            q_copies.append(put("q", b * seq + d, sq.at[peer, b], rq.at[z, b], z_peer(d)))
    rq[z] = sq[z]

    frame_valid = jnp.concatenate(
        [valid_rows(start, size) for j, start, size, _ in steps for b in range(2)], axis=0
    )

    def spread(origin):
        at = pl.ds(pl.multiple_of(origin * frame, frame), frame)
        both = kv[at, :]
        one = jnp.where(low, jnp.ones_like(both), both)
        vx[at, :] = jnp.where(frame_valid, one, jnp.zeros_like(one))

    spread(z)
    for d in range(1, seq):
        for k in range(len(steps)):
            kv_copies[k * (seq - 1) + d - 1].wait_recv()
        spread(lax.rem(z + seq - d, seq))

    mine = place * seq + z

    def q_copy(d, b):
        origin = lax.rem(z + seq - d, seq)
        return remote("q", b * seq + d, sq.at[0, b], rq.at[origin, b], z_peer(d))

    def o_copy(d, b):
        origin = lax.rem(z + seq - d, seq)
        device = (s, origin, b // 2, b % 2)
        return remote("o", d * 4 + b, so.at[d, b], ro.at[mine], device, mine)

    def each_o(d, b, act):
        itself = jnp.logical_and(d == 0, place == b)

        @pl.when(jnp.logical_not(itself))
        def _():
            act(o_copy(d, b))

    @pl.loop(0, seq)
    def _(d):
        origin = lax.rem(z + seq - d, seq)
        for b in range(4):

            @pl.when(d > 0)
            def _():
                q_copy(d, b).wait_recv()

        for b in range(4):
            packed = rq[origin, b].astype(F32)
            q = jnp.concatenate([packed, swap(packed)], axis=0)
            q = jnp.where(low, q, 0.0).astype(BF)
            scores = dot_t(q, kv[...])
            probs = jnp.exp2(scores - jnp.max(scores, axis=-1, keepdims=True))
            mixed = mm(probs.astype(BF), vx[...])
            out = mixed / jnp.where(low, 1.0, swap(mixed))
            so[d, b] = jnp.where(low, swap(out)[:half], out[half:]).astype(BF)
            each_o(d, b, lambda copy: copy.start())

    ro_own = so[0, place]
    ro[mine] = ro_own
    go_x.wait_recv()
    go_f = put("go", 1, go.at[go_from], go.at[go_from], core)
    for copy in late_loads:
        copy.wait()
    for slot in range(4 * seq):

        @pl.when(slot != mine)
        def _():
            remote("o", 0, so.at[0, 0], ro.at[slot], core, slot).wait_recv()

    for i in range(2 * seq):
        at = pl.ds(i * LANES, LANES)
        even, odd = ro[2 * i].astype(F32), ro[2 * i + 1].astype(F32)
        pair = [jnp.where(low, even, swap(odd)), jnp.where(low, swap(even), odd)]
        a2[:, at] = jnp.concatenate(pair, axis=0).astype(BF)
    first = fst[...].astype(F32)
    go_f.wait_recv()
    second = (first + mm(a2[...], go[...])).astype(BF).astype(F32)
    stacked = jnp.concatenate([first, second], axis=-1)
    n3 = layer_norm(stacked, h_gain[...], head_eps).astype(BF)
    pj[...] = (mm(n3, wp[...]) + h_bias[...]).astype(BF)

    after = lax.rem(place + 1, 4)
    before = lax.rem(place + 3, 4)

    def frame_peer(index):
        return (s, z, index // 2, lax.rem(index, 2))

    start = (real - width) // TILE * TILE
    slab = halo.shape[1]
    down = put(
        "halo", 0, pj.at[pl.ds(start, rows - start)], halo.at[0, pl.ds(0, rows - start)],
        frame_peer(after),
    )
    upward = put("halo", 1, pj.at[pl.ds(0, slab)], halo.at[1], frame_peer(before))
    stage[0:rows, :] = second
    for r in range(height):
        blocks_ref[0, r] = stage[r * width : (r + 1) * width, :].astype(BF)
    base = 8
    xbuf[...] = jnp.zeros_like(xbuf)
    xbuf[base + width : base + width + real, :] = pj[...].astype(F32)[:real]
    down.wait_recv()
    upward.wait_recv()
    skip = real - width - start
    lower = jnp.where(place > 0, halo[0].astype(F32), 0.0)
    upper = jnp.where(place < 3, halo[1].astype(F32), 0.0)
    xbuf[base : base + width, :] = lower[skip : skip + width]
    xbuf[base + width + real : base + 2 * width + real, :] = upper[:width]
    col = lax.rem(lax.broadcasted_iota(jnp.int32, (rows, 1), 0), width)
    channels = pj.shape[1]
    total = jnp.zeros((rows, channels), F32)
    for i in range(3):
        for j in range(3):
            first_row = base + width * i + j - 1
            window = xbuf[first_row : first_row + rows, :]
            if j == 0:
                window = jnp.where(col > 0, window, 0.0)
            if j == 2:
                window = jnp.where(col < width - 1, window, 0.0)
            total = total + mm(window.astype(BF), wc[3 * i + j])
    stage[0:rows, 0:channels] = total
    for r in range(height):
        feat_ref[0, r] = stage[r * width : (r + 1) * width, 0:channels].astype(BF)

    for copy in started:
        copy.wait_send()

    @pl.loop(0, seq)
    def _(d):
        for b in range(4):
            each_o(d, b, lambda copy: copy.wait_send())


def scene_program(seq, *arrays):
    (tokens, f_gain, f_qkv, f_out, g_gain, g_qkv, g_out, h_gain, h_proj, h_bias, h_conv) = arrays
    height, width, dim = tokens.shape[1:]
    real = height * width
    rows = up(real)
    cols = f_qkv.shape[2] // 2
    pairs = cols // LANES
    channels = h_proj.shape[1]
    frame = 4 * rows
    half = rows // 2
    most = row_parts(rows)[0][1]
    vmem = pl.BlockSpec(memory_space=pltpu.VMEM)
    hbm = pl.BlockSpec(memory_space=pl.ANY)
    start = (real - width) // TILE * TILE
    slab = max(up(width), rows - start)
    _, copies = sem_layout(seq, pairs)
    return pl.pallas_call(
        functools.partial(scene_kernel, seq, height, width),
        out_shape=(
            jax.ShapeDtypeStruct(tokens.shape, BF),
            jax.ShapeDtypeStruct((1, height, width, channels), BF),
        ),
        in_specs=[vmem, vmem, hbm, hbm, vmem, hbm, hbm, vmem, hbm, vmem, hbm],
        out_specs=(vmem, vmem),
        scratch_shapes=[
            pltpu.VMEM((rows, dim), F32),
            pltpu.VMEM((4, rows, dim), BF),
            pltpu.VMEM((3, dim, cols), BF),
            pltpu.VMEM((3, dim, cols), BF),
            pltpu.VMEM((dim, 2 * cols), BF),
            pltpu.VMEM((dim, 2 * cols), BF),
            pltpu.VMEM((2 * cols, dim), BF),
            pltpu.VMEM((4 * cols, dim), BF),
            pltpu.VMEM(h_proj.shape, BF),
            pltpu.VMEM((9, channels, channels), BF),
            pltpu.VMEM((frame, cols), BF),
            pltpu.VMEM((frame, 2 * cols), BF),
            pltpu.VMEM((frame, 2 * cols), BF),
            pltpu.VMEM((4, 2, most, cols), BF),
            pltpu.VMEM((4, most, cols), BF),
            pltpu.VMEM((4, most, dim), F32),
            pltpu.VMEM((4, most, dim), BF),
            pltpu.VMEM((4, most, dim), BF),
            pltpu.VMEM((4, most, dim), BF),
            pltpu.VMEM((4, most, dim), BF),
            pltpu.VMEM((rows, dim), BF),
            pltpu.VMEM((4, rows, cols), F32),
            pltpu.VMEM((seq, frame, LANES), BF),
            pltpu.VMEM((seq * frame, LANES), BF),
            pltpu.VMEM((seq * frame, LANES), BF),
            pltpu.VMEM((seq, 4, half, LANES), BF),
            pltpu.VMEM((seq, 4, half, LANES), BF),
            pltpu.VMEM((seq, 4, half, LANES), BF),
            pltpu.VMEM((4 * seq, half, LANES), BF),
            pltpu.VMEM((rows, 4 * cols), BF),
            pltpu.VMEM((rows, channels), BF),
            pltpu.VMEM((2, slab, channels), BF),
            pltpu.VMEM((up(rows + 2 * width + 2 * TILE), channels), F32),
            pltpu.SemaphoreType.DMA((copies,)),
            pltpu.SemaphoreType.DMA((copies,)),
            pltpu.SemaphoreType.DMA((5 + 4 * pairs,)),
        ],
        compiler_params=pltpu.CompilerParams(collective_id=0, has_side_effects=True),
    )(
        tokens,
        f_gain.reshape(1, -1),
        f_qkv,
        f_out,
        g_gain.reshape(1, -1),
        g_qkv,
        g_out,
        h_gain.reshape(1, -1),
        h_proj,
        h_bias.reshape(1, -1),
        h_conv.reshape(9, channels, channels),
    )


def routed(mesh, *arrays):
    sizes = mesh.shape
    frames, height, width = arrays[0].shape[:3]
    heads = arrays[2].shape[2] // HD
    fits = (
        sizes["head"] == 2
        and sizes["band"] == 2
        and frames == 1
        and heads == 2 * sizes["seq"]
        and sizes["seq"] % 2 == 0
        and arrays[0].shape[3] == 2 * arrays[2].shape[2]
        and arrays[10].shape[2] <= arrays[0].shape[3]
        and height * width >= up(width)
        and up(height * width) >= 2 * TILE
    )
    if fits:
        return scene_program(sizes["seq"], *arrays)
    return on_device(*arrays)


def solution(mesh):
    return jax.shard_map(
        functools.partial(routed, mesh),
        mesh=mesh,
        in_specs=(
            P(("scene", "seq"), ("head", "band"), None, None),
            P(),
            P(None, None, "head"),
            P("head", None),
            P(),
            P(None, None, "head"),
            P("head", None),
            P(),
            P(),
            P(),
            P(),
        ),
        out_specs=(
            P(("scene", "seq"), ("head", "band"), None, None),
            P(("scene", "seq"), ("head", "band"), None, None),
        ),
        check_vma=False,
    )
```

time: 71.7 us -> 66.2 us (0.923)
  Pallas kernels: 65.9 us -> 62.2 us
  local copies, waits for them, and re-layouts: 4.17 us -> 3.11 us
    reshape x3 -> x0, local copies, waits for them, and re-layouts: 4.16 us -> none  [the longest x1 1.69 us: scene_program(): blocks[:real].reshape(tokens.shape)]
    pallas_call x1, Pallas kernels: 65.9 us -> 62.2 us  [scene_program(): pl.pallas_call(functools.partial(scene_kernel, seq, height, width), out_s...]
    unnamed x0 -> x2, local copies, waits for them, and re-layouts: none -> 3.11 us
where the time goes in v1:
time: 66.2 us; the launch traced here: 66 us
  Pallas kernels  62.2 us (94%)
  local copies, waits for them, and re-layouts  3.11 us (5%)
    pallas_call x1, Pallas kernels, scene_program(): pl.pallas_call(functools.partial(scene_kernel, seq, height, width), out_s...  62.2 us
    unnamed x2, local copies, waits for them, and re-layouts  3.11 us

profile of v1, /device:TPU:0, one launch (start us, length us, event | category | flops | bytes accessed | tf_op | source)
XLA Modules:
  0.0 66.0 jit_solution(388949883943268398)
XLA Ops:
  0.6 62.2 %shard_map.122 = (bf16[1,3,37,1024]{3,2,1,0:T(8,128)(2,1)}, bf16[1,3,37,256]{3,2,1,0:T(8,128)(2,1)}) custom-call(bf16[1,3,37,1024]{3,2,1,0:T(8,128)(2,1)} %tok_ref.1, f32[1,1024]{1,0:T(1,128)} %bitcast.7, bf16[3,1024,512]{2,1,0:T(8,128)(2,1)} %f_qkv.1, bf16[512,1024]{1,0:T(8,128)(2,1)} %f_out.1, f32[1,1024]{1,0:T(1,128)} %bitcast.8, ...), custom_call_target="tpu_custom_call" | custom-call | tf_op jit(solution)/shard_map/pallas_call | solution.py:662
  62.9 1.7 %copy.15 = bf16[1,3,37,1024]{3,2,1,0:T(8,128)(2,1)} copy(bf16[1,3,37,1024]{3,2,1,0:T(8,128)(2,1)} %get-tuple-element.4) | data formatting | bytes 454656
  64.5 1.5 %copy.16 = bf16[1,3,37,256]{3,2,1,0:T(8,128)(2,1)} copy(bf16[1,3,37,256]{3,2,1,0:T(8,128)(2,1)} %get-tuple-element.5) | data formatting | bytes 113664

commit v2 on v1

--- a/solution.py
+++ b/solution.py
@@ -242,19 +242,24 @@
     seq,
     height,
     width,
-    tok_ref,
-    f_gain,
+    tok_hbm,
+    f_gain_hbm,
     f_qkv,
     f_out,
-    g_gain,
+    g_gain_hbm,
     g_qkv,
     g_out,
-    h_gain,
+    h_gain_hbm,
     h_proj,
-    h_bias,
+    h_bias_hbm,
     h_conv,
     blocks_ref,
     feat_ref,
+    tok_ref,
+    f_gain,
+    g_gain,
+    h_gain,
+    h_bias,
     stage,
     toks,
     wf,
@@ -306,8 +311,12 @@
     core, across = (s, z, x, 1 - c), (s, z, 1 - x, c)
     place = 2 * x + c
 
-    def z_peer(offset):
-        return (s, lax.rem(z + offset, seq), x, c)
+    def paired(k):
+        bits = [1 << i for i in range(seq.bit_length()) if k >> i & 1]
+        return z + sum(bit - 2 * bit * lax.rem(lax.div(z, bit), 2) for bit in bits)
+
+    def z_peer(k):
+        return (s, paired(k), x, c)
 
     def remote(name, index, source, target, device, back=None):
         return pltpu.make_async_remote_copy(
@@ -319,6 +328,13 @@
             device_id_type=pl.DeviceIdType.MESH,
         )
 
+    barrier = pltpu.get_barrier_semaphore()
+    everyone = [core, across, (s, z, 1 - x, 1 - c)] + [z_peer(d) for d in range(1, seq)]
+    for device in everyone:
+        pl.semaphore_signal(
+            barrier, inc=1, device_id=device, device_id_type=pl.DeviceIdType.MESH
+        )
+
     started = []
 
     def put(name, index, source, target, device):
@@ -336,6 +352,8 @@
         loads.append(copy)
         return copy
 
+    tok_load = load(tok_hbm, tok_ref)
+    f_gain_load = load(f_gain_hbm, f_gain)
     wf_load = load(f_qkv.at[:, :, own_cols], wf)
     fo_loads = []
     for r in range(2):
@@ -345,14 +363,11 @@
             fo_loads.append(load(source, fo.at[pl.ds(r * cols + (i ^ 1) * HD, HD)]))
     wg_load = load(g_qkv.at[:, :, own_cols], wg)
     half_rows = pl.ds(pl.multiple_of(x * 2 * cols, 2 * cols), 2 * cols)
+    g_gain_load = load(g_gain_hbm, g_gain)
     late_loads = [load(g_out, go.at[half_rows]), load(h_proj, wp), load(h_conv, wc)]
-
-    barrier = pltpu.get_barrier_semaphore()
-    everyone = [core, across, (s, z, 1 - x, 1 - c)] + [z_peer(d) for d in range(1, seq)]
-    for device in everyone:
-        pl.semaphore_signal(
-            barrier, inc=1, device_id=device, device_id_type=pl.DeviceIdType.MESH
-        )
+    late_loads += [load(h_gain_hbm, h_gain), load(h_bias_hbm, h_bias)]
+
+    tok_load.wait()
     for r in range(height):
         stage[r * width : (r + 1) * width, :] = tok_ref[0, r].astype(F32)
     for r in range(real, rows):
@@ -374,6 +389,7 @@
     def valid_rows(start, size):
         return lax.broadcasted_iota(jnp.int32, (size, 1), 0) + start < real
 
+    f_gain_load.wait()
     wf_load.wait()
     for p in range(pairs):
         at = pl.ds(p * LANES, LANES)
@@ -393,6 +409,7 @@
     qkv1(0, 0, rows, place)
     tok_core.wait_recv()
     qkv1(1, 0, rows, 2 * x + 1 - c)
+    g_gain_load.wait()
     wg_load.wait()
     for p in range(pairs):
         at = pl.ds(p * LANES, LANES)
@@ -460,8 +477,7 @@
         n_own[k, at] = layer_norm(first.astype(F32), g_gain[...], norm_eps).astype(BF)
         n_copies.append(put("norm", k, n_own.at[k, at], n_in.at[k, at], core))
 
-    kv_copies, q_copies = [], []
-    base_row = pl.multiple_of(z * frame, frame)
+    kv_copies = [[] for _ in range(seq)]
 
     def qkv2(k):
         j, start, size, offset = steps[k]
@@ -472,11 +488,9 @@
         for h in range(2 * pairs):
             skv[h, pl.ds(offset, 2 * size), :] = both[:, h * LANES : (h + 1) * LANES]
         to = pl.ds(pl.multiple_of(z * frame + offset, TILE), 2 * size)
-        for d in range(1, seq):
-            peer = lax.rem(z + d, seq)
-            kv_copies.append(
-                put("kv", k * seq + d, skv.at[peer, pl.ds(offset, 2 * size)], kv.at[to], z_peer(d))
-            )
+        for d in reversed(range(1, seq)):
+            source = skv.at[paired(d), pl.ds(offset, 2 * size)]
+            kv_copies[d].append(put("kv", k * seq + d, source, kv.at[to], z_peer(d)))
         kv[to, :] = skv[z, pl.ds(offset, 2 * size), :]
         queries = mm(n, wg[0]) * QSCALE
         q2[2 * j + c, pl.ds(start, size), :] = queries[:size]
@@ -485,33 +499,25 @@
     for copy in fo_loads:
         copy.wait()
     attend(0)
-    attend(1)
     project(0)
-    attend(2)
-    project(1)
-    attend(3)
-    project(2)
-    project(3)
+    for k in range(1, len(steps)):
+        attend(k)
+        project(k)
     go_part = pl.ds(pl.multiple_of(x * 2 * cols + c * cols, cols), cols)
     go_from = pl.ds(pl.multiple_of((1 - x) * 2 * cols + c * cols, cols), cols)
     go_x = put("go", 0, g_out.at[own_cols], go.at[go_part], across)
-    norm2(0)
-    norm2(1)
-    qkv2(0)
-    qkv2(1)
-    norm2(2)
-    norm2(3)
-    qkv2(2)
-    qkv2(3)
+    for k in range(len(steps)):
+        norm2(k)
+        qkv2(k)
     for b in range(4):
         for p in range(pairs):
             tile = q2[b, :, pl.ds(p * LANES, LANES)]
             top, under = tile[:half], tile[half:]
             sq[2 * p, b] = jnp.where(low, top, swap(under)).astype(BF)
             sq[2 * p + 1, b] = jnp.where(low, swap(top), under).astype(BF)
-        for d in range(1, seq):
-            peer = lax.rem(z + d, seq)
-            q_copies.append(put("q", b * seq + d, sq.at[peer, b], rq.at[z, b], z_peer(d)))
+    for d in range(1, seq):
+        for b in range(4):
+            put("q", b * seq + d, sq.at[paired(d), b], rq.at[z, b], z_peer(d))
     rq[z] = sq[z]
 
     frame_valid = jnp.concatenate(
@@ -526,47 +532,59 @@
 
     spread(z)
     for d in range(1, seq):
-        for k in range(len(steps)):
-            kv_copies[k * (seq - 1) + d - 1].wait_recv()
-        spread(lax.rem(z + seq - d, seq))
+        for copy in kv_copies[d]:
+            copy.wait_recv()
+        spread(paired(d))
 
     mine = place * seq + z
 
-    def q_copy(d, b):
-        origin = lax.rem(z + seq - d, seq)
-        return remote("q", b * seq + d, sq.at[0, b], rq.at[origin, b], z_peer(d))
-
-    def o_copy(d, b):
-        origin = lax.rem(z + seq - d, seq)
+    def q_copy(d, b, origin):
+        device = (s, origin, x, c)
+        return remote("q", b * seq + d, sq.at[0, b], rq.at[origin, b], device)
+
+    def o_copy(d, b, origin):
         device = (s, origin, b // 2, b % 2)
         return remote("o", d * 4 + b, so.at[d, b], ro.at[mine], device, mine)
 
-    def each_o(d, b, act):
+    def origin_of(d):
+        origin = z
+        for i in range((seq - 1).bit_length()):
+            bit = 1 << i
+            flip = lax.rem(lax.div(d, bit), 2)
+            origin = origin + flip * (bit - 2 * bit * lax.rem(lax.div(z, bit), 2))
+        return origin
+
+    def each_o(d, b, origin, act):
         itself = jnp.logical_and(d == 0, place == b)
 
         @pl.when(jnp.logical_not(itself))
         def _():
-            act(o_copy(d, b))
+            act(o_copy(d, b, origin))
 
     @pl.loop(0, seq)
     def _(d):
-        origin = lax.rem(z + seq - d, seq)
+        origin = origin_of(d)
         for b in range(4):
 
             @pl.when(d > 0)
             def _():
-                q_copy(d, b).wait_recv()
-
-        for b in range(4):
-            packed = rq[origin, b].astype(F32)
-            q = jnp.concatenate([packed, swap(packed)], axis=0)
-            q = jnp.where(low, q, 0.0).astype(BF)
+                q_copy(d, b, origin).wait_recv()
+
+        for pair in range(2):
+            q = []
+            for b in (2 * pair, 2 * pair + 1):
+                packed = rq[origin, b].astype(F32)
+                q += [packed, swap(packed)]
+            q = jnp.where(low, jnp.concatenate(q, axis=0), 0.0).astype(BF)
             scores = dot_t(q, kv[...])
             probs = jnp.exp2(scores - jnp.max(scores, axis=-1, keepdims=True))
             mixed = mm(probs.astype(BF), vx[...])
             out = mixed / jnp.where(low, 1.0, swap(mixed))
-            so[d, b] = jnp.where(low, swap(out)[:half], out[half:]).astype(BF)
-            each_o(d, b, lambda copy: copy.start())
+            for i in range(2):
+                b = 2 * pair + i
+                o = out[i * rows : (i + 1) * rows]
+                so[d, b] = jnp.where(low, swap(o)[:half], o[half:]).astype(BF)
+                each_o(d, b, origin, lambda copy: copy.start())
 
     ro_own = so[0, place]
     ro[mine] = ro_own
@@ -640,7 +658,7 @@
     @pl.loop(0, seq)
     def _(d):
         for b in range(4):
-            each_o(d, b, lambda copy: copy.wait_send())
+            each_o(d, b, origin_of(d), lambda copy: copy.wait_send())
 
 
 def scene_program(seq, *arrays):
@@ -655,7 +673,7 @@
     half = rows // 2
     most = row_parts(rows)[0][1]
     vmem = pl.BlockSpec(memory_space=pltpu.VMEM)
-    hbm = pl.BlockSpec(memory_space=pl.ANY)
+    hbm = pl.BlockSpec(memory_space=pltpu.HBM)
     start = (real - width) // TILE * TILE
     slab = max(up(width), rows - start)
     _, copies = sem_layout(seq, pairs)
@@ -665,9 +683,14 @@
             jax.ShapeDtypeStruct(tokens.shape, BF),
             jax.ShapeDtypeStruct((1, height, width, channels), BF),
         ),
-        in_specs=[vmem, vmem, hbm, hbm, vmem, hbm, hbm, vmem, hbm, vmem, hbm],
+        in_specs=[hbm] * 11,
         out_specs=(vmem, vmem),
         scratch_shapes=[
+            pltpu.VMEM(tokens.shape, BF),
+            pltpu.VMEM((1, dim), F32),
+            pltpu.VMEM((1, dim), F32),
+            pltpu.VMEM((1, 2 * dim), F32),
+            pltpu.VMEM((1, channels), F32),
             pltpu.VMEM((rows, dim), F32),
             pltpu.VMEM((4, rows, dim), BF),
             pltpu.VMEM((3, dim, cols), BF),
@@ -703,21 +726,28 @@
             pltpu.VMEM((up(rows + 2 * width + 2 * TILE), channels), F32),
             pltpu.SemaphoreType.DMA((copies,)),
             pltpu.SemaphoreType.DMA((copies,)),
-            pltpu.SemaphoreType.DMA((5 + 4 * pairs,)),
+            pltpu.SemaphoreType.DMA((10 + 4 * pairs,)),
         ],
-        compiler_params=pltpu.CompilerParams(collective_id=0, has_side_effects=True),
+        compiler_params=pltpu.CompilerParams(
+            collective_id=0, has_side_effects=True, vmem_limit_bytes=40 * 2**20
+        ),
     )(
-        tokens,
-        f_gain.reshape(1, -1),
-        f_qkv,
-        f_out,
-        g_gain.reshape(1, -1),
-        g_qkv,
-        g_out,
-        h_gain.reshape(1, -1),
-        h_proj,
-        h_bias.reshape(1, -1),
-        h_conv.reshape(9, channels, channels),
+        *[
+            pltpu.with_memory_space_constraint(array, pltpu.HBM)
+            for array in (
+                tokens,
+                f_gain.reshape(1, -1),
+                f_qkv,
+                f_out,
+                g_gain.reshape(1, -1),
+                g_qkv,
+                g_out,
+                h_gain.reshape(1, -1),
+                h_proj,
+                h_bias.reshape(1, -1),
+                h_conv.reshape(9, channels, channels),
+            )
+        ]
     )
 
 
@@ -730,7 +760,8 @@
         and sizes["band"] == 2
         and frames == 1
         and heads == 2 * sizes["seq"]
-        and sizes["seq"] % 2 == 0
+        and sizes["seq"] & (sizes["seq"] - 1) == 0
+        and sizes["seq"] >= 2
         and arrays[0].shape[3] == 2 * arrays[2].shape[2]
         and arrays[10].shape[2] <= arrays[0].shape[3]
         and height * width >= up(width)

time: 66.2 us -> 60.1 us (0.908)
  Pallas kernels: 62.2 us -> 58 us
  local copies, waits for them, and re-layouts: 3.11 us -> 1.32 us
    pallas_call x1, Pallas kernels: 62.2 us -> 58 us  [scene_program(): pl.pallas_call(functools.partial(scene_kernel, seq, height, width), out_s...]
    unnamed x2, local copies, waits for them, and re-layouts: 3.11 us -> 1.32 us
where the time goes in v2:
time: 60.1 us; the launch traced here: 60 us
  Pallas kernels  58 us (97%)
  local copies, waits for them, and re-layouts  1.32 us (2%)
  between operations  0.64 us (1%)
    pallas_call x1, Pallas kernels, scene_program(): pl.pallas_call(functools.partial(scene_kernel, seq, height, width), out_s...  58 us
    unnamed x2, local copies, waits for them, and re-layouts  1.32 us

profile of v2, /device:TPU:0, one launch (start us, length us, event | category | flops | bytes accessed | tf_op | source)
XLA Modules:
  0.0 60.0 jit_solution(1764832778360557399)
XLA Ops:
  0.6 58.0 %shard_map.122 = (bf16[1,3,37,1024]{3,2,1,0:T(8,128)(2,1)S(1)}, bf16[1,3,37,256]{3,2,1,0:T(8,128)(2,1)S(1)}) custom-call(bf16[1,3,37,1024]{3,2,1,0:T(8,128)(2,1)} %tok_hbm.1, f32[1,1024]{1,0:T(1,128)} %bitcast.7, bf16[3,1024,512]{2,1,0:T(8,128)(2,1)} %f_qkv.1, bf16[512,1024]{1,0:T(8,128)(2,1)} %f_out.1, f32[1,1024]{1,0:T(1,128)} %bitcast.8, ...), custom_call_target="tpu_custom_call" | custom-call | tf_op jit(solution)/shard_map/pallas_call | solution.py:680
  58.7 0.7 %copy.15 = bf16[1,3,37,1024]{3,2,1,0:T(8,128)(2,1)} copy(bf16[1,3,37,1024]{3,2,1,0:T(8,128)(2,1)S(1)} %get-tuple-element.4) | data formatting | bytes 454656
  59.4 0.6 %copy.16 = bf16[1,3,37,256]{3,2,1,0:T(8,128)(2,1)} copy(bf16[1,3,37,256]{3,2,1,0:T(8,128)(2,1)S(1)} %get-tuple-element.5) | data formatting | bytes 113664

commit v3 on v2

--- a/solution.py
+++ b/solution.py
@@ -220,7 +220,8 @@
 def step_list(rows):
     steps, at = [], 0
     for j in range(2):
-        for start, size in row_parts(rows):
+        long, short = (size for _, size in row_parts(rows))
+        for start, size in [(0, short), (short, long)] if j == 0 else [(0, long), (long, short)]:
             steps.append((j, start, size, at))
             at += 2 * size
     return steps
@@ -429,27 +430,28 @@
 
     att_copies, p_copies, n_copies = [], [], []
 
-    def attend(k):
+    def attend(k, p):
         j, start, size, _ = steps[k]
-        for p in range(pairs):
-            at = pl.ds(p * LANES, LANES)
-            qp = jnp.concatenate(
-                [q1[pl.ds((2 * j + b) * rows + start, size), at] for b in range(2)], axis=0
-            )
-            mixed = []
-            for e in range(2):
-                tile = pl.ds((2 * p + e) * LANES, LANES)
-                zero = jnp.zeros_like(qp)
-                lhs = jnp.where(low, qp, zero) if e == 0 else jnp.where(low, zero, qp)
-                scores = dot_t(lhs, kv1[:, tile])
-                probs = jnp.exp2(scores - jnp.max(scores, axis=-1, keepdims=True))
-                mixed.append(mm(probs.astype(BF), vx1[:, tile]))
-            top = jnp.where(low, mixed[1], mixed[0])
-            bottom = swap(jnp.where(low, mixed[0], mixed[1]))
-            out = (top / bottom).astype(BF)
-            for b in range(2):
-                att[k, b, pl.ds(0, size), at] = out[b * size : (b + 1) * size]
-        at = pl.ds(0, size)
+        at = pl.ds(p * LANES, LANES)
+        qp = jnp.concatenate(
+            [q1[pl.ds((2 * j + b) * rows + start, size), at] for b in range(2)], axis=0
+        )
+        mixed = []
+        for e in range(2):
+            tile = pl.ds((2 * p + e) * LANES, LANES)
+            zero = jnp.zeros_like(qp)
+            lhs = jnp.where(low, qp, zero) if e == 0 else jnp.where(low, zero, qp)
+            scores = dot_t(lhs, kv1[:, tile])
+            probs = jnp.exp2(scores - jnp.max(scores, axis=-1, keepdims=True))
+            mixed.append(mm(probs.astype(BF), vx1[:, tile]))
+        top = jnp.where(low, mixed[1], mixed[0])
+        bottom = swap(jnp.where(low, mixed[0], mixed[1]))
+        out = (top / bottom).astype(BF)
+        for b in range(2):
+            att[k, b, pl.ds(0, size), at] = out[b * size : (b + 1) * size]
+
+    def send_att(k):
+        at = pl.ds(0, steps[k][2])
         att_copies.append(put("att", k, att.at[k, 1 - c, at], att_in.at[k, at], core))
 
     def project(k):
@@ -488,7 +490,7 @@
         for h in range(2 * pairs):
             skv[h, pl.ds(offset, 2 * size), :] = both[:, h * LANES : (h + 1) * LANES]
         to = pl.ds(pl.multiple_of(z * frame + offset, TILE), 2 * size)
-        for d in reversed(range(1, seq)):
+        for d in range(1, seq):
             source = skv.at[paired(d), pl.ds(offset, 2 * size)]
             kv_copies[d].append(put("kv", k * seq + d, source, kv.at[to], z_peer(d)))
         kv[to, :] = skv[z, pl.ds(offset, 2 * size), :]
@@ -498,11 +500,16 @@
 
     for copy in fo_loads:
         copy.wait()
-    attend(0)
-    project(0)
+    for p in range(pairs):
+        attend(0, p)
+    send_att(0)
     for k in range(1, len(steps)):
-        attend(k)
-        project(k)
+        for p in range(pairs):
+            attend(k, p)
+            if p == 0:
+                project(k - 1)
+        send_att(k)
+    project(len(steps) - 1)
     go_part = pl.ds(pl.multiple_of(x * 2 * cols + c * cols, cols), cols)
     go_from = pl.ds(pl.multiple_of((1 - x) * 2 * cols + c * cols, cols), cols)
     go_x = put("go", 0, g_out.at[own_cols], go.at[go_part], across)
@@ -515,9 +522,10 @@
             top, under = tile[:half], tile[half:]
             sq[2 * p, b] = jnp.where(low, top, swap(under)).astype(BF)
             sq[2 * p + 1, b] = jnp.where(low, swap(top), under).astype(BF)
-    for d in range(1, seq):
-        for b in range(4):
-            put("q", b * seq + d, sq.at[paired(d), b], rq.at[z, b], z_peer(d))
+    for pair in range(2):
+        for d in range(1, seq):
+            for b in (2 * pair, 2 * pair + 1):
+                put("q", b * seq + d, sq.at[paired(d), b], rq.at[z, b], z_peer(d))
     rq[z] = sq[z]
 
     frame_valid = jnp.concatenate(
@@ -542,8 +550,9 @@
         device = (s, origin, x, c)
         return remote("q", b * seq + d, sq.at[0, b], rq.at[origin, b], device)
 
-    def o_copy(d, b, origin):
-        device = (s, origin, b // 2, b % 2)
+    def o_copy(d, pair, i, origin):
+        b = 2 * pair + i
+        device = (s, origin, pair, i)
         return remote("o", d * 4 + b, so.at[d, b], ro.at[mine], device, mine)
 
     def origin_of(d):
@@ -554,37 +563,36 @@
             origin = origin + flip * (bit - 2 * bit * lax.rem(lax.div(z, bit), 2))
         return origin
 
-    def each_o(d, b, origin, act):
-        itself = jnp.logical_and(d == 0, place == b)
+    def each_o(d, pair, i, origin, act):
+        itself = jnp.logical_and(d == 0, place == 2 * pair + i)
 
         @pl.when(jnp.logical_not(itself))
         def _():
-            act(o_copy(d, b, origin))
-
-    @pl.loop(0, seq)
-    def _(d):
+            act(o_copy(d, pair, i, origin))
+
+    @pl.loop(0, 2 * seq)
+    def _(turn):
+        pair, d = lax.div(turn, seq), lax.rem(turn, seq)
         origin = origin_of(d)
-        for b in range(4):
+        for i in range(2):
 
             @pl.when(d > 0)
             def _():
-                q_copy(d, b, origin).wait_recv()
-
-        for pair in range(2):
-            q = []
-            for b in (2 * pair, 2 * pair + 1):
-                packed = rq[origin, b].astype(F32)
-                q += [packed, swap(packed)]
-            q = jnp.where(low, jnp.concatenate(q, axis=0), 0.0).astype(BF)
-            scores = dot_t(q, kv[...])
-            probs = jnp.exp2(scores - jnp.max(scores, axis=-1, keepdims=True))
-            mixed = mm(probs.astype(BF), vx[...])
-            out = mixed / jnp.where(low, 1.0, swap(mixed))
-            for i in range(2):
-                b = 2 * pair + i
-                o = out[i * rows : (i + 1) * rows]
-                so[d, b] = jnp.where(low, swap(o)[:half], o[half:]).astype(BF)
-                each_o(d, b, origin, lambda copy: copy.start())
+                q_copy(d, 2 * pair + i, origin).wait_recv()
+
+        q = []
+        for i in range(2):
+            packed = rq[origin, 2 * pair + i].astype(F32)
+            q += [packed, swap(packed)]
+        q = jnp.where(low, jnp.concatenate(q, axis=0), 0.0).astype(BF)
+        scores = dot_t(q, kv[...])
+        probs = jnp.exp2(scores - jnp.max(scores, axis=-1, keepdims=True))
+        mixed = mm(probs.astype(BF), vx[...])
+        out = mixed / jnp.where(low, 1.0, swap(mixed))
+        for i in range(2):
+            o = out[i * rows : (i + 1) * rows]
+            so[d, 2 * pair + i] = jnp.where(low, swap(o)[:half], o[half:]).astype(BF)
+            each_o(d, pair, i, origin, lambda copy: copy.start())
 
     ro_own = so[0, place]
     ro[mine] = ro_own
@@ -658,7 +666,7 @@
     @pl.loop(0, seq)
     def _(d):
         for b in range(4):
-            each_o(d, b, origin_of(d), lambda copy: copy.wait_send())
+            each_o(d, b // 2, b % 2, origin_of(d), lambda copy: copy.wait_send())
 
 
 def scene_program(seq, *arrays):

time: 60.1 us -> 57.3 us (0.953)
  Pallas kernels: 58 us -> 55.1 us
    pallas_call x1, Pallas kernels: 58 us -> 55.1 us  [scene_program(): pl.pallas_call(functools.partial(scene_kernel, seq, height, width), out_s...]
where the time goes in v3:
time: 57.3 us; the launch traced here: 57.1 us
  Pallas kernels  55.1 us (96%)
  local copies, waits for them, and re-layouts  1.32 us (2%)
  between operations  0.64 us (1%)
    pallas_call x1, Pallas kernels, scene_program(): pl.pallas_call(functools.partial(scene_kernel, seq, height, width), out_s...  55.1 us
    unnamed x2, local copies, waits for them, and re-layouts  1.32 us

profile of v3, /device:TPU:0, one launch (start us, length us, event | category | flops | bytes accessed | tf_op | source)
XLA Modules:
  0.0 57.1 jit_solution(1790163153704802479)
XLA Ops:
  0.6 55.1 %shard_map.122 = (bf16[1,3,37,1024]{3,2,1,0:T(8,128)(2,1)S(1)}, bf16[1,3,37,256]{3,2,1,0:T(8,128)(2,1)S(1)}) custom-call(bf16[1,3,37,1024]{3,2,1,0:T(8,128)(2,1)} %tok_hbm.1, f32[1,1024]{1,0:T(1,128)} %bitcast.7, bf16[3,1024,512]{2,1,0:T(8,128)(2,1)} %f_qkv.1, bf16[512,1024]{1,0:T(8,128)(2,1)} %f_out.1, f32[1,1024]{1,0:T(1,128)} %bitcast.8, ...), custom_call_target="tpu_custom_call" | custom-call | tf_op jit(solution)/shard_map/pallas_call | solution.py:688
  55.8 0.7 %copy.15 = bf16[1,3,37,1024]{3,2,1,0:T(8,128)(2,1)} copy(bf16[1,3,37,1024]{3,2,1,0:T(8,128)(2,1)S(1)} %get-tuple-element.4) | data formatting | bytes 454656
  56.5 0.6 %copy.16 = bf16[1,3,37,256]{3,2,1,0:T(8,128)(2,1)} copy(bf16[1,3,37,256]{3,2,1,0:T(8,128)(2,1)S(1)} %get-tuple-element.5) | data formatting | bytes 113664

commit v4 on v3

--- a/solution.py
+++ b/solution.py
@@ -193,6 +193,7 @@
 F32 = jnp.float32
 TILE = 16
 LANES = 2 * HD
+STEP_SHARES = ((3, 4), (4, 3))
 QSCALE = HD ** (-0.5) * math.log2(math.e)
 
 
@@ -217,20 +218,30 @@
     return [(0, first), (first, rows - first)]
 
 
+def split_rows(rows, shares):
+    units, sizes = rows // TILE, []
+    for i, share in enumerate(shares):
+        left = units - sum(sizes)
+        size = left if i == len(shares) - 1 else max(1, units * share // sum(shares))
+        sizes.append(size)
+    return [size * TILE for size in sizes if size > 0]
+
+
 def step_list(rows):
     steps, at = [], 0
-    for j in range(2):
-        long, short = (size for _, size in row_parts(rows))
-        for start, size in [(0, short), (short, long)] if j == 0 else [(0, long), (long, short)]:
+    for j, shares in enumerate(STEP_SHARES):
+        start = 0
+        for size in split_rows(rows, shares):
             steps.append((j, start, size, at))
             at += 2 * size
+            start += size
     return steps
 
 
-def sem_layout(seq, pairs):
+def sem_layout(seq, count):
     names = [
-        ("tok", 1), ("tok_x", 2), ("tok_f", 2), ("att", 4), ("part", 4), ("norm", 4),
-        ("kv", 4 * seq), ("q", 4 * seq), ("o", 4 * seq), ("go", 2), ("halo", 2),
+        ("tok", 1), ("tok_x", 2), ("tok_f", 2), ("att", count), ("part", count), ("norm", count),
+        ("kv", count * seq), ("q", 4 * seq), ("o", 4 * seq), ("go", 2), ("halo", 2),
     ]
     at, table = 0, {}
     for name, size in names:
@@ -308,7 +319,7 @@
     half = rows // 2
     steps = step_list(rows)
     parts = row_parts(rows)
-    sems, _ = sem_layout(seq, pairs)
+    sems, _ = sem_layout(seq, len(steps))
     core, across = (s, z, x, 1 - c), (s, z, 1 - x, c)
     place = 2 * x + c
 
@@ -524,8 +535,8 @@
             sq[2 * p + 1, b] = jnp.where(low, swap(top), under).astype(BF)
     for pair in range(2):
         for d in range(1, seq):
-            for b in (2 * pair, 2 * pair + 1):
-                put("q", b * seq + d, sq.at[paired(d), b], rq.at[z, b], z_peer(d))
+            bands = pl.ds(2 * pair, 2)
+            put("q", pair * seq + d, sq.at[paired(d), bands], rq.at[z, bands], z_peer(d))
     rq[z] = sq[z]
 
     frame_valid = jnp.concatenate(
@@ -546,9 +557,9 @@
 
     mine = place * seq + z
 
-    def q_copy(d, b, origin):
-        device = (s, origin, x, c)
-        return remote("q", b * seq + d, sq.at[0, b], rq.at[origin, b], device)
+    def q_copy(d, pair, origin):
+        device, bands = (s, origin, x, c), pl.ds(2 * pair, 2)
+        return remote("q", pair * seq + d, sq.at[0, bands], rq.at[origin, bands], device)
 
     def o_copy(d, pair, i, origin):
         b = 2 * pair + i
@@ -570,29 +581,33 @@
         def _():
             act(o_copy(d, pair, i, origin))
 
-    @pl.loop(0, 2 * seq)
+    @pl.loop(0, 2 * seq // 2)
     def _(turn):
-        pair, d = lax.div(turn, seq), lax.rem(turn, seq)
-        origin = origin_of(d)
-        for i in range(2):
+        pair = lax.div(turn, seq // 2)
+        group = lax.rem(turn, seq // 2)
+        group = group + pair * (seq // 2 - 1 - 2 * group)
+        ds = [2 * group + i for i in range(2)]
+        origins = [origin_of(d) for d in ds]
+        for d, origin in zip(ds, origins):
 
             @pl.when(d > 0)
             def _():
-                q_copy(d, 2 * pair + i, origin).wait_recv()
-
-        q = []
-        for i in range(2):
-            packed = rq[origin, 2 * pair + i].astype(F32)
-            q += [packed, swap(packed)]
-        q = jnp.where(low, jnp.concatenate(q, axis=0), 0.0).astype(BF)
-        scores = dot_t(q, kv[...])
-        probs = jnp.exp2(scores - jnp.max(scores, axis=-1, keepdims=True))
-        mixed = mm(probs.astype(BF), vx[...])
-        out = mixed / jnp.where(low, 1.0, swap(mixed))
-        for i in range(2):
-            o = out[i * rows : (i + 1) * rows]
-            so[d, 2 * pair + i] = jnp.where(low, swap(o)[:half], o[half:]).astype(BF)
-            each_o(d, pair, i, origin, lambda copy: copy.start())
+                q_copy(d, pair, origin).wait_recv()
+
+        for d, origin in zip(ds, origins):
+            q = []
+            for i in range(2):
+                packed = rq[origin, 2 * pair + i].astype(F32)
+                q += [packed, swap(packed)]
+            q = jnp.where(low, jnp.concatenate(q, axis=0), 0.0).astype(BF)
+            scores = dot_t(q, kv[...])
+            probs = jnp.exp2(scores - jnp.max(scores, axis=-1, keepdims=True))
+            mixed = mm(probs.astype(BF), vx[...])
+            out = mixed / jnp.where(low, 1.0, swap(mixed))
+            for i in range(2):
+                o = out[i * rows : (i + 1) * rows]
+                so[d, 2 * pair + i] = jnp.where(low, swap(o)[:half], o[half:]).astype(BF)
+                each_o(d, pair, i, origin, lambda copy: copy.start())
 
     ro_own = so[0, place]
     ro[mine] = ro_own
@@ -679,12 +694,12 @@
     channels = h_proj.shape[1]
     frame = 4 * rows
     half = rows // 2
-    most = row_parts(rows)[0][1]
+    count, most = len(step_list(rows)), max(step[2] for step in step_list(rows))
     vmem = pl.BlockSpec(memory_space=pltpu.VMEM)
     hbm = pl.BlockSpec(memory_space=pltpu.HBM)
     start = (real - width) // TILE * TILE
     slab = max(up(width), rows - start)
-    _, copies = sem_layout(seq, pairs)
+    _, copies = sem_layout(seq, count)
     return pl.pallas_call(
         functools.partial(scene_kernel, seq, height, width),
         out_shape=(
@@ -712,13 +727,13 @@
             pltpu.VMEM((frame, cols), BF),
             pltpu.VMEM((frame, 2 * cols), BF),
             pltpu.VMEM((frame, 2 * cols), BF),
-            pltpu.VMEM((4, 2, most, cols), BF),
-            pltpu.VMEM((4, most, cols), BF),
-            pltpu.VMEM((4, most, dim), F32),
-            pltpu.VMEM((4, most, dim), BF),
-            pltpu.VMEM((4, most, dim), BF),
-            pltpu.VMEM((4, most, dim), BF),
-            pltpu.VMEM((4, most, dim), BF),
+            pltpu.VMEM((count, 2, most, cols), BF),
+            pltpu.VMEM((count, most, cols), BF),
+            pltpu.VMEM((count, most, dim), F32),
+            pltpu.VMEM((count, most, dim), BF),
+            pltpu.VMEM((count, most, dim), BF),
+            pltpu.VMEM((count, most, dim), BF),
+            pltpu.VMEM((count, most, dim), BF),
             pltpu.VMEM((rows, dim), BF),
             pltpu.VMEM((4, rows, cols), F32),
             pltpu.VMEM((seq, frame, LANES), BF),

time: 57.3 us -> 56.5 us (0.986)
  Pallas kernels: 55.1 us -> 54.4 us
    pallas_call x1, Pallas kernels: 55.1 us -> 54.4 us  [scene_program(): pl.pallas_call(functools.partial(scene_kernel, seq, height, width), out_s...]
where the time goes in v4:
time: 56.5 us; the launch traced here: 56.4 us
  Pallas kernels  54.4 us (96%)
  local copies, waits for them, and re-layouts  1.32 us (2%)
  between operations  0.64 us (1%)
    pallas_call x1, Pallas kernels, scene_program(): pl.pallas_call(functools.partial(scene_kernel, seq, height, width), out_s...  54.4 us
    unnamed x2, local copies, waits for them, and re-layouts  1.32 us

profile of v4, /device:TPU:0, one launch (start us, length us, event | category | flops | bytes accessed | tf_op | source)
XLA Modules:
  0.0 56.4 jit_solution(16924666147487534269)
XLA Ops:
  0.6 54.4 %shard_map.122 = (bf16[1,3,37,1024]{3,2,1,0:T(8,128)(2,1)S(1)}, bf16[1,3,37,256]{3,2,1,0:T(8,128)(2,1)S(1)}) custom-call(bf16[1,3,37,1024]{3,2,1,0:T(8,128)(2,1)} %tok_hbm.1, f32[1,1024]{1,0:T(1,128)} %bitcast.7, bf16[3,1024,512]{2,1,0:T(8,128)(2,1)} %f_qkv.1, bf16[512,1024]{1,0:T(8,128)(2,1)} %f_out.1, f32[1,1024]{1,0:T(1,128)} %bitcast.8, ...), custom_call_target="tpu_custom_call" | custom-call | tf_op jit(solution)/shard_map/pallas_call | solution.py:703
  55.1 0.7 %copy.15 = bf16[1,3,37,1024]{3,2,1,0:T(8,128)(2,1)} copy(bf16[1,3,37,1024]{3,2,1,0:T(8,128)(2,1)S(1)} %get-tuple-element.4) | data formatting | bytes 454656
  55.8 0.6 %copy.16 = bf16[1,3,37,256]{3,2,1,0:T(8,128)(2,1)} copy(bf16[1,3,37,256]{3,2,1,0:T(8,128)(2,1)S(1)} %get-tuple-element.5) | data formatting | bytes 113664

commit v5 on v4

--- a/solution.py
+++ b/solution.py
@@ -193,7 +193,7 @@
 F32 = jnp.float32
 TILE = 16
 LANES = 2 * HD
-STEP_SHARES = ((3, 4), (4, 3))
+STEP_SHARES = ((3, 4), (5, 2))
 QSCALE = HD ** (-0.5) * math.log2(math.e)
 
 

time: 56.5 us -> 56 us (level)
  no operation moved by 1% of the time
where the time goes in v5:
time: 56 us; the launch traced here: 55.9 us
  Pallas kernels  53.9 us (96%)
  local copies, waits for them, and re-layouts  1.32 us (2%)
  between operations  0.64 us (1%)
    pallas_call x1, Pallas kernels, scene_program(): pl.pallas_call(functools.partial(scene_kernel, seq, height, width), out_s...  53.9 us
    unnamed x2, local copies, waits for them, and re-layouts  1.32 us

profile of v5, /device:TPU:0, one launch (start us, length us, event | category | flops | bytes accessed | tf_op | source)
XLA Modules:
  0.0 55.9 jit_solution(1965357285677300431)
XLA Ops:
  0.6 53.9 %shard_map.122 = (bf16[1,3,37,1024]{3,2,1,0:T(8,128)(2,1)S(1)}, bf16[1,3,37,256]{3,2,1,0:T(8,128)(2,1)S(1)}) custom-call(bf16[1,3,37,1024]{3,2,1,0:T(8,128)(2,1)} %tok_hbm.1, f32[1,1024]{1,0:T(1,128)} %bitcast.7, bf16[3,1024,512]{2,1,0:T(8,128)(2,1)} %f_qkv.1, bf16[512,1024]{1,0:T(8,128)(2,1)} %f_out.1, f32[1,1024]{1,0:T(1,128)} %bitcast.8, ...), custom_call_target="tpu_custom_call" | custom-call | tf_op jit(solution)/shard_map/pallas_call | solution.py:703
  54.6 0.7 %copy.15 = bf16[1,3,37,1024]{3,2,1,0:T(8,128)(2,1)} copy(bf16[1,3,37,1024]{3,2,1,0:T(8,128)(2,1)S(1)} %get-tuple-element.4) | data formatting | bytes 454656
  55.3 0.6 %copy.16 = bf16[1,3,37,256]{3,2,1,0:T(8,128)(2,1)} copy(bf16[1,3,37,256]{3,2,1,0:T(8,128)(2,1)S(1)} %get-tuple-element.5) | data formatting | bytes 113664

commit v6 on v5

--- a/solution.py
+++ b/solution.py
@@ -193,7 +193,7 @@
 F32 = jnp.float32
 TILE = 16
 LANES = 2 * HD
-STEP_SHARES = ((3, 4), (5, 2))
+STEP_SHARES = ((3, 4), (6, 1))
 QSCALE = HD ** (-0.5) * math.log2(math.e)
 
 

time: 56 us -> 55.9 us (level)
  no operation moved by 1% of the time
where the time goes in v6:
time: 55.9 us; the launch traced here: 55.7 us
  Pallas kernels  53.8 us (96%)
  local copies, waits for them, and re-layouts  1.32 us (2%)
  between operations  0.64 us (1%)
    pallas_call x1, Pallas kernels, scene_program(): pl.pallas_call(functools.partial(scene_kernel, seq, height, width), out_s...  53.8 us
    unnamed x2, local copies, waits for them, and re-layouts  1.32 us

profile of v6, /device:TPU:0, one launch (start us, length us, event | category | flops | bytes accessed | tf_op | source)
XLA Modules:
  0.0 55.7 jit_solution(3002544204251262620)
XLA Ops:
  0.6 53.8 %shard_map.122 = (bf16[1,3,37,1024]{3,2,1,0:T(8,128)(2,1)S(1)}, bf16[1,3,37,256]{3,2,1,0:T(8,128)(2,1)S(1)}) custom-call(bf16[1,3,37,1024]{3,2,1,0:T(8,128)(2,1)} %tok_hbm.1, f32[1,1024]{1,0:T(1,128)} %bitcast.7, bf16[3,1024,512]{2,1,0:T(8,128)(2,1)} %f_qkv.1, bf16[512,1024]{1,0:T(8,128)(2,1)} %f_out.1, f32[1,1024]{1,0:T(1,128)} %bitcast.8, ...), custom_call_target="tpu_custom_call" | custom-call | tf_op jit(solution)/shard_map/pallas_call | solution.py:703
  54.4 0.7 %copy.15 = bf16[1,3,37,1024]{3,2,1,0:T(8,128)(2,1)} copy(bf16[1,3,37,1024]{3,2,1,0:T(8,128)(2,1)S(1)} %get-tuple-element.4) | data formatting | bytes 454656
  55.1 0.6 %copy.16 = bf16[1,3,37,256]{3,2,1,0:T(8,128)(2,1)} copy(bf16[1,3,37,256]{3,2,1,0:T(8,128)(2,1)S(1)} %get-tuple-element.5) | data formatting | bytes 113664

commit v7 on v6

--- a/solution.py
+++ b/solution.py
@@ -193,7 +193,7 @@
 F32 = jnp.float32
 TILE = 16
 LANES = 2 * HD
-STEP_SHARES = ((3, 4), (6, 1))
+STEP_SHARES = ((2, 5), (6, 1))
 QSCALE = HD ** (-0.5) * math.log2(math.e)
 
 

time: 55.9 us -> 56.2 us (level)
  no operation moved by 1% of the time
where the time goes in v7:
time: 56.2 us; the launch traced here: 56.1 us
  Pallas kernels  54.1 us (96%)
  local copies, waits for them, and re-layouts  1.32 us (2%)
  between operations  0.64 us (1%)
    pallas_call x1, Pallas kernels, scene_program(): pl.pallas_call(functools.partial(scene_kernel, seq, height, width), out_s...  54.1 us
    unnamed x2, local copies, waits for them, and re-layouts  1.32 us

profile of v7, /device:TPU:0, one launch (start us, length us, event | category | flops | bytes accessed | tf_op | source)
XLA Modules:
  0.0 56.1 jit_solution(8701291151796073808)
XLA Ops:
  0.6 54.1 %shard_map.122 = (bf16[1,3,37,1024]{3,2,1,0:T(8,128)(2,1)S(1)}, bf16[1,3,37,256]{3,2,1,0:T(8,128)(2,1)S(1)}) custom-call(bf16[1,3,37,1024]{3,2,1,0:T(8,128)(2,1)} %tok_hbm.1, f32[1,1024]{1,0:T(1,128)} %bitcast.7, bf16[3,1024,512]{2,1,0:T(8,128)(2,1)} %f_qkv.1, bf16[512,1024]{1,0:T(8,128)(2,1)} %f_out.1, f32[1,1024]{1,0:T(1,128)} %bitcast.8, ...), custom_call_target="tpu_custom_call" | custom-call | tf_op jit(solution)/shard_map/pallas_call | solution.py:703
  54.8 0.7 %copy.15 = bf16[1,3,37,1024]{3,2,1,0:T(8,128)(2,1)} copy(bf16[1,3,37,1024]{3,2,1,0:T(8,128)(2,1)S(1)} %get-tuple-element.4) | data formatting | bytes 454656
  55.4 0.6 %copy.16 = bf16[1,3,37,256]{3,2,1,0:T(8,128)(2,1)} copy(bf16[1,3,37,256]{3,2,1,0:T(8,128)(2,1)S(1)} %get-tuple-element.5) | data formatting | bytes 113664
